TPU v7x, 256 devices: a whole 4x4x8 slice. The times are simulated.
256 devices in a mesh: dom: 8 (over z), lat: 32 (over y, x, core).
Axes of the slice: x: 4, y: 4, z: 8, core: 2. Of those that a mesh axis runs over, the one named last changes fastest.
Arguments:
- ensemble: float32 [16, 3, 256, 4096], P('dom', None, 'lat'), may hold values from -6 to 6
- perturbation: float32 [16, 3, 256, 4096], P('dom', None, 'lat'), may hold values from -4 to 4
- parents: int32 [16], replicated, may hold values from 0 to 15, as said below
- depth: float32 [256, 4096], P('lat'), may hold values from 0.5 to 2
Outputs:
- forecast: float32 [16, 3, 256, 4096], P('dom', None, 'lat')
Inputs may be any that keep to these rules, and one draw needn't show every extreme that they name: parents[j] is the member whose fields the new member j copies; every aligned block of 2 members holds a member that some entry names.
All inputs are finite; a program needn't handle non-finite values.
Results may differ from a plain program's by a relative error of at most 0.00014.
Values sent between devices are 32-bit elements; how exact they have to be, the bound alone decides.
No kernel may reach another device: no remote copies, remote signals or barrier semaphores. Data moves between devices by JAX's collectives and lax.ppermute only.
A program may use at most 128 MiB of HBM per device.

v0:
```python
import jax
import jax.numpy as jnp
from jax import lax
from jax.experimental import pallas as pl
from jax.experimental.pallas import tpu as pltpu
from jax.sharding import PartitionSpec as P

STEPS = 4
STEPS_PER_EXCHANGE = 2
TIME_STEP = 0.8
LANES = 128
SUBLANES = 8
REACH = 4 * STEPS_PER_EXCHANGE
ROUNDS = 4
CHAINS = 2
UNROLL = 32
VMEM_LIMIT = 16 * 2**20


def to_tiles(strip):
    *lead, rows, lon = strip.shape
    split = strip.reshape(*lead, rows, lon // LANES, LANES)
    return jnp.swapaxes(split, -3, -2).reshape(*lead, lon // LANES * rows, LANES)


def from_tiles(tiles, rows):
    *lead, count, _ = tiles.shape
    split = tiles.reshape(*lead, count // rows, rows, LANES)
    return jnp.swapaxes(split, -3, -2).reshape(*lead, rows, count // rows * LANES)


def neighbour(value, axis, shift, wrap=False):
    devices = lax.axis_size(axis)
    pairs = [(i, (i + shift) % devices) for i in range(devices) if wrap or 0 <= i + shift < devices]
    return lax.ppermute(value, axis, pairs)


def both_sides(value):
    return neighbour(value, "lat", 1), neighbour(value, "lat", -1)


def where_row(row, chunk, rows, chunks):
    return pl.ds(chunk * rows + row, SUBLANES, stride=chunks * rows)


def choose(table_ref, row, identities, candidates):
    wanted = table_ref[row]
    value = candidates[0]
    for identity, candidate in zip(identities[1:], candidates[1:]):
        value = jnp.where(wanted == table_ref[identity], candidate, value)
    return value


def plan_kernel(devices, per, rounds, me_ref, parents_ref, table_ref, case_ref):
    count = devices * per
    pairs = 2 * count
    half = devices // 2
    me = me_ref[0]
    down_row = lax.broadcasted_iota(jnp.int32, (pairs, LANES), 0)
    along_row = lax.broadcasted_iota(jnp.int32, (pairs, LANES), 1)

    def facts(index):
        item = lax.rem(index, count)
        return index // count, item, item // per

    sides = [facts(index) for index in (down_row, along_row)]
    far = [jnp.zeros((pairs, LANES), jnp.int32) for _ in range(2)]
    for entry in range(count):
        parent = parents_ref[entry]
        origin = parent // per
        hops = lax.rem(entry // per - origin + devices, devices)
        goes_up = jnp.logical_or(hops < half, jnp.logical_and(hops == half, lax.rem(origin, 2) == 0))
        slot = parent + jnp.where(goes_up, 0, count)
        distance = jnp.where(goes_up, hops, devices - hops)
        far = [jnp.maximum(f, jnp.where(index == slot, distance, 0)) for f, index in zip(far, (down_row, along_row))]

    def put(row, value):
        table_ref[row] = jnp.broadcast_to(value, (SUBLANES, LANES)).astype(jnp.int32)

    for k in range(per):
        put(k, jnp.full((SUBLANES, LANES), me * per + k, jnp.int32))
        put(per + k, jnp.full((SUBLANES, LANES), parents_ref[me * per + k], jnp.int32))
    position = [jnp.zeros((pairs, LANES), jnp.int32) for _ in range(2)]
    unmet = []
    for r in range(rounds):
        left, link, key = [], [], []
        for (direction, item, origin), f, p, index in zip(sides, far, position, (down_row, along_row)):
            step = jnp.where(direction == 0, p, devices - p)
            left.append(f - p)
            link.append(lax.rem(origin + step, devices) + direction * devices)
            key.append(jnp.where(f > p, (f - p) * pairs + pairs - 1 - index, -1))
        same = link[0] == link[1]
        beaten_down = jnp.max(jnp.where(same & (key[1] > key[0]), 1, 0), axis=1, keepdims=True)
        beaten_along = jnp.max(jnp.where(same & (key[0] > key[1]), 1, 0), axis=0, keepdims=True)
        wins = [
            jnp.where((left[0] > 0) & (jnp.broadcast_to(beaten_down, left[0].shape) == 0), 1, 0),
            jnp.where((left[1] > 0) & (jnp.broadcast_to(beaten_along, left[1].shape) == 0), 1, 0),
        ]
        for q, (place, direction) in enumerate(((me, 0), (me + devices - 1, 0), (me, 1), (me + 1, 1))):
            here = (wins[1] > 0) & (link[1] == lax.rem(place, devices) + direction * devices)
            put(2 * per + 4 * r + q, jnp.max(jnp.where(here, sides[1][1], -1)[:SUBLANES], axis=1, keepdims=True))
        position = [p + w for p, w in zip(position, wins)]
        unmet.append(jnp.max(jnp.where(far[1] > position[1], 1, 0)[:SUBLANES], axis=1, keepdims=True))
    case_ref[...] = jnp.broadcast_to(unmet[-2] + unmet[-1], (SUBLANES, LANES))


def plan(parents, me, devices, per, rounds):
    smem = pl.BlockSpec(memory_space=pltpu.SMEM)
    vmem = pl.BlockSpec(memory_space=pltpu.VMEM)
    return pl.pallas_call(
        lambda *refs: plan_kernel(devices, per, rounds, *refs),
        out_shape=(
            jax.ShapeDtypeStruct((2 * per + 4 * rounds, SUBLANES, LANES), jnp.int32),
            jax.ShapeDtypeStruct((SUBLANES, LANES), jnp.int32),
        ),
        in_specs=[smem, smem],
        out_specs=(vmem, vmem),
        compiler_params=pltpu.CompilerParams(vmem_limit_bytes=VMEM_LIMIT),
        name="plan",
    )(me, parents)


def candidates_of(per, own_ref, received, field, base, rows):
    values = [own_ref[k, field, pl.ds(base, rows), :].reshape(-1, SUBLANES, LANES) for k in range(per)]
    return values + [ref[field].reshape(-1, SUBLANES, LANES) for ref in received]


def select_kernel(per, base, round_index, table_ref, own_ref, *refs):
    received, (up_ref, down_ref) = refs[:-2], refs[-2:]
    fields, rows, _ = up_ref.shape
    names = identity_rows(per, len(received))
    for f in range(fields):
        values = candidates_of(per, own_ref, received, f, base, rows)
        for out_ref, q in ((up_ref, 0), (down_ref, 2)):
            out_ref[f] = choose(table_ref, 2 * per + 4 * round_index + q, names, values).reshape(rows, LANES)


def identity_rows(per, received):
    return list(range(per)) + [2 * per + 4 * (k // 2) + (1, 3)[k % 2] for k in range(received)]


def select(table, own, received, base, rows, round_index):
    per, fields = own.shape[:2]
    vmem = pl.BlockSpec(memory_space=pltpu.VMEM)
    shape = jax.ShapeDtypeStruct((fields, rows, LANES), jnp.float32)
    return pl.pallas_call(
        lambda *refs: select_kernel(per, base, round_index, *refs),
        out_shape=(shape, shape),
        in_specs=[vmem] * (2 + len(received)),
        out_specs=(vmem, vmem),
        cost_estimate=pl.CostEstimate(flops=0, bytes_accessed=4 * fields * rows * LANES * 4, transcendentals=0),
        compiler_params=pltpu.CompilerParams(vmem_limit_bytes=VMEM_LIMIT),
        name="select",
    )(table, own, *received)


def spread(rows, value_ref, out_ref):
    fields = out_ref.shape[0]
    chunks = out_ref.shape[-1] // LANES

    def one_row(r, carry):
        for f in range(fields):
            for c in range(chunks):
                out_ref[f, r, :, pl.ds(c * LANES, LANES)] = value_ref[f, where_row(r, c, rows, chunks), :]
        return carry

    lax.fori_loop(0, rows, one_row, 0)


def collect_kernel(per, rows, entry, chains, table_ref, own_ref, noise_ref, *refs):
    out_ref, value_ref = refs[-2:]
    received = refs[:-2]
    each = len(received) // chains
    fields, count, _ = value_ref.shape
    part = count // chains
    names = identity_rows(per, each)
    for f in range(fields):
        for h in range(chains):
            values = candidates_of(per, own_ref, received[h * each:(h + 1) * each], f, h * part, part)
            found = choose(table_ref, per + entry, names, values).reshape(part, LANES)
            where = pl.ds(h * part, part)
            value_ref[f, where, :] = found + noise_ref[entry, f, where, :]
    spread(rows, value_ref, out_ref)


def collect(table, own, noise, chains, rows, entry):
    per, fields, count, _ = own.shape
    lon = count // rows * LANES
    vmem = pl.BlockSpec(memory_space=pltpu.VMEM)
    pieces = [piece for chain in chains for piece in chain]
    return pl.pallas_call(
        lambda *refs: collect_kernel(per, rows, entry, len(chains), *refs),
        out_shape=jax.ShapeDtypeStruct((fields, rows, SUBLANES, lon // SUBLANES), jnp.float32),
        in_specs=[vmem] * (3 + len(pieces)),
        out_specs=vmem,
        scratch_shapes=[pltpu.VMEM((fields, count, LANES), jnp.float32)],
        cost_estimate=pl.CostEstimate(flops=fields * rows * lon, bytes_accessed=12 * fields * rows * lon, transcendentals=0),
        compiler_params=pltpu.CompilerParams(vmem_limit_bytes=VMEM_LIMIT),
        name="collect",
    )(table, own, noise, *pieces)


def unpack_rows(rows, source):
    fields, count, _ = source.shape
    lon = count // rows * LANES
    vmem = pl.BlockSpec(memory_space=pltpu.VMEM)
    return pl.pallas_call(
        lambda *refs: spread(rows, *refs),
        out_shape=jax.ShapeDtypeStruct((fields, rows, SUBLANES, lon // SUBLANES), jnp.float32),
        in_specs=[vmem],
        out_specs=vmem,
        cost_estimate=pl.CostEstimate(flops=0, bytes_accessed=8 * fields * rows * lon, transcendentals=0),
        compiler_params=pltpu.CompilerParams(vmem_limit_bytes=VMEM_LIMIT),
        name="unpack",
    )(source)


def advance_kernel(rows, total_rows, final, place_ref, before, own, after, d_before, d_own, d_after, out_ref, state, first, second, third, depth):
    chunks = state.shape[-1] // LANES
    base_row = place_ref[0] * rows - REACH
    lane = lax.broadcasted_iota(jnp.int32, (SUBLANES, LANES), 1)
    at_start, at_end = lane == 0, lane == LANES - 1

    def lanes(c):
        return pl.ds(c * LANES, LANES)

    def load_row(ref, *index):
        return [ref[(*index, slice(None), lanes(c))] for c in range(chunks)]

    def difference_east(row):
        right = [pltpu.roll(v, 1, 1) for v in row]
        left = [pltpu.roll(v, LANES - 1, 1) for v in row]
        before_ = [pltpu.roll(right[-1], 1, 0)] + right[:-1]
        after_ = left[1:] + [pltpu.roll(left[0], SUBLANES - 1, 0)]
        return [
            jnp.where(at_start, b, r) - jnp.where(at_end, a, l)
            for b, r, a, l in zip(before_, right, after_, left)
        ]

    for block, (strip, d) in enumerate(((before, d_before), (own, d_own), (after, d_after))):
        state[:, block * rows:(block + 1) * rows] = strip[...]
        depth[block * rows:(block + 1) * rows] = d[...]

    def stage(source, low, high, emit):
        def flux(r):
            return [d * v for d, v in zip(load_row(depth, r), load_row(source, 2, r))]

        def one(r, carry):
            h_before, h_here, f_before, f_here = carry
            h_after, f_after = load_row(source, 0, r + 1), flux(r + 1)
            east, north = load_row(source, 1, r), load_row(source, 2, r)
            row = base_row + r
            turn = 0.8 * ((2 * row + 1).astype(jnp.float32) * (1.0 / total_rows) - 1.0)
            inside = jnp.logical_and(row >= 0, row < total_rows)
            dx_flux = difference_east([a * b for a, b in zip(load_row(depth, r), east)])
            dx_h = difference_east(h_here)
            rate_h = [x + (a - b) for x, a, b in zip(dx_flux, f_before, f_after)]
            rate_u = [x + turn * v for x, v in zip(dx_h, north)]
            rate_v = [(a - b) - turn * u for a, b, u in zip(h_before, h_after, east)]
            emit(r, inside, (rate_h, rate_u, rate_v))
            return h_here, h_after, f_here, f_after

        def several(count):
            def run(r, carry):
                for k in range(count):
                    carry = one(r + k, carry)
                return carry
            return run

        carry = (load_row(source, 0, low - 1), load_row(source, 0, low), flux(low - 1), flux(low))
        trips, rest = divmod(high - low, UNROLL)
        carry = lax.fori_loop(0, trips, lambda i, c: several(UNROLL)(low + UNROLL * i, c), carry)
        several(rest)(high - rest, carry)

    def advance(target, weight):
        def emit(r, inside, rates):
            scale = jnp.where(inside, jnp.float32(weight), jnp.float32(0.0))
            for f, rate in enumerate(rates):
                for c in range(chunks):
                    target[f, r, :, lanes(c)] = state[f, r, :, lanes(c)] + scale * rate[c]
        return emit

    def finish(last):
        def emit(r, inside, rates):
            scale = jnp.where(inside, jnp.float32(TIME_STEP / 12.0), jnp.float32(0.0))
            third_part = jnp.float32(1.0 / 3.0)
            for f, rate in enumerate(rates):
                for c in range(chunks):
                    y, a, b, d = (ref[f, r, :, lanes(c)] for ref in (state, first, second, third))
                    value = ((a - y) + (b + b + d)) * third_part + scale * rate[c]
                    if not last:
                        state[f, r, :, lanes(c)] = value
                    elif final:
                        out_ref[f, where_row(r - REACH, c, rows, chunks), :] = value
                    else:
                        out_ref[f, r - REACH, :, lanes(c)] = value
        return emit

    low, high = 0, 2 * REACH + rows
    for step in range(STEPS_PER_EXCHANGE):
        stage(state, low + 1, high - 1, advance(first, 0.25 * TIME_STEP))
        stage(first, low + 2, high - 2, advance(second, 0.25 * TIME_STEP))
        stage(second, low + 3, high - 3, advance(third, 0.5 * TIME_STEP))
        stage(third, low + 4, high - 4, finish(step == STEPS_PER_EXCHANGE - 1))
        low, high = low + 4, high - 4


def advance(strips, depth_strips, place, total_rows, final=None):
    fields, rows, _, width = strips[0].shape
    reach_rows = 2 * REACH + rows
    plane = pltpu.VMEM((fields, reach_rows, SUBLANES, width), jnp.float32)
    vmem = pl.BlockSpec(memory_space=pltpu.VMEM)
    smem = pl.BlockSpec(memory_space=pltpu.SMEM)
    operands = [place, *strips, *depth_strips]
    in_specs = [smem] + [vmem] * 6
    options = {}
    if final is None:
        out_shape, out_specs = strips[0].shape, vmem
    else:
        member, members, partial = final
        count = rows * SUBLANES * width // LANES
        out_shape = (members, fields, count, LANES)
        out_specs = pl.BlockSpec((None, fields, count, LANES), lambda i: (member, 0, 0, 0))
        if partial is not None:
            operands.append(partial)
            in_specs.append(pl.BlockSpec(memory_space=pl.ANY))
            options["input_output_aliases"] = {7: 0}

    def kernel(*refs):
        advance_kernel(rows, total_rows, final is not None, *refs[:7], *refs[-6:])

    return pl.pallas_call(
        kernel,
        grid=(1,),
        out_shape=jax.ShapeDtypeStruct(out_shape, jnp.float32),
        in_specs=in_specs,
        out_specs=out_specs,
        scratch_shapes=[plane] * 4 + [pltpu.VMEM((reach_rows, SUBLANES, width), jnp.float32)],
        compiler_params=pltpu.CompilerParams(vmem_limit_bytes=VMEM_LIMIT),
        cost_estimate=pl.CostEstimate(
            flops=8 * 24 * reach_rows * SUBLANES * width, bytes_accessed=5 * 4 * fields * rows * SUBLANES * width, transcendentals=0
        ),
        name="advance",
        **options,
    )(*operands)


def body(ensemble, perturbation, parents, depth):
    per, fields, rows, lon = ensemble.shape
    total_rows = rows * lax.axis_size("lat")
    devices = lax.axis_size("dom")
    me = lax.axis_index("dom").astype(jnp.int32)
    place = lax.axis_index("lat").astype(jnp.int32)[None]
    table, case = plan(parents, me[None], devices, per, ROUNDS + 1)
    tiles = to_tiles(ensemble)
    noise = to_tiles(perturbation)
    count = tiles.shape[2]
    part = count // CHAINS

    def exchange(chains, round_index):
        sends = [select(table, tiles, chain, h * part, part, round_index) for h, chain in enumerate(chains)]
        return [
            chain + [neighbour(up, "dom", 1, True), neighbour(down, "dom", -1, True)]
            for chain, (up, down) in zip(chains, sends)
        ]

    depth_rows = unpack_rows(rows, to_tiles(depth)[None])[0]
    depth_before, depth_after = both_sides(depth_rows)

    chains = [[] for _ in range(CHAINS)]
    for round_index in range(ROUNDS):
        chains = exchange(chains, round_index)
        if round_index == 1:
            chains, depth_before, depth_after = lax.optimization_barrier((chains, depth_before, depth_after))
    depth_strips = (depth_before, depth_rows, depth_after)

    def gather(chains):
        return tuple(collect(table, tiles, noise, chains, rows, k) for k in range(per))

    def all_round(chains):
        own_parents = lax.dynamic_slice_in_dim(parents, me * per, per, 0)

        def turn(k, carry):
            block, found = carry
            block = neighbour(block, "dom", 1, True)
            owner = (me + devices - k - 1) % devices
            found = tuple(
                jnp.where(own_parents[e] // per == owner, block[own_parents[e] % per], found[e]) for e in range(per)
            )
            return block, found

        start = tuple(tiles[own_parents[e] % per] for e in range(per))
        found = lax.fori_loop(0, devices - 1, turn, (tiles, start))[1]
        return tuple(unpack_rows(rows, found[k] + noise[k]) for k in range(per))

    states = lax.switch(
        case[0, 0], [gather, lambda chains: gather(exchange(chains, ROUNDS)), all_round], chains
    )
    for _ in range(STEPS // STEPS_PER_EXCHANGE - 1):
        sides = [both_sides(state) for state in states]
        states = [
            advance((before, state, after), depth_strips, place, total_rows)
            for state, (before, after) in zip(states, sides)
        ]
    result = None
    for member, state in enumerate(states):
        before, after = both_sides(state)
        result = advance((before, state, after), depth_strips, place, total_rows, (member, per, result))
    return from_tiles(result, rows)


def solution(mesh):
    placed = (P("dom", None, "lat", None), P("dom", None, "lat", None), P(), P("lat", None))
    return jax.shard_map(
        body, mesh=mesh, in_specs=placed, out_specs=P("dom", None, "lat", None), check_vma=False
    )
```

profile of v0, /device:TPU:88, one launch (start us, length us, event | category | flops | bytes accessed | tf_op | source)
XLA Modules:
  0.0 100.7 jit_solution(11194438310577824390)
XLA Ops:
  3.4 2.0 %collective-permute-start.9 = (f32[3,128,128]{2,1,0:T(8,128)S(1)}, f32[3,128,128]{2,1,0:T(8,128)S(1)}, u32[]{:S(2)}, u32[]{:S(2)}) collective-permute-start(f32[3,128,128]{2,1,0:T(8,128)S(1)} %get-tuple-element.660), channel_id=1, source_target_pairs={{0,32},{32,64},{64,96},{96,128},{128,160},{160,192},{192,224},{224... | collective-permute-start | bytes 589832 | tf_op jit(solution)/shard_map/ppermute | solution.py:35
  5.5 3.1 %collective-permute-start.5 = (f32[3,128,128]{2,1,0:T(8,128)S(1)}, f32[3,128,128]{2,1,0:T(8,128)S(1)}, u32[]{:S(2)}, u32[]{:S(2)}) collective-permute-start(f32[3,128,128]{2,1,0:T(8,128)S(1)} %get-tuple-element.656), channel_id=1, source_target_pairs={{0,32},{32,64},{64,96},{96,128},{128,160},{160,192},{192,224},{224... | collective-permute-start | bytes 589832 | tf_op jit(solution)/shard_map/ppermute | solution.py:35
  8.8 3.7 %collective-permute-start.14 = (f32[8,8,512]{2,1,0:T(8,128)S(1)}, f32[8,8,512]{2,1,0:T(8,128)S(1)}, u32[]{:S(2)}, u32[]{:S(2)}) collective-permute-start(f32[8,8,512]{2,1,0:T(8,128)S(1)} %bitcast.40), channel_id=1, source_target_pairs={{1,0},{2,1},{3,2},{4,3},{5,4},{6,5},{7,6},{8,7},{9,8},{10,9},{11,1... | collective-permute-start | bytes 393224 | tf_op jit(solution)/shard_map/ppermute | solution.py:35
  14.3 3.3 %collective-permute-start.11 = (f32[3,128,128]{2,1,0:T(8,128)S(1)}, f32[3,128,128]{2,1,0:T(8,128)S(1)}, u32[]{:S(2)}, u32[]{:S(2)}) collective-permute-start(f32[3,128,128]{2,1,0:T(8,128)S(1)} %get-tuple-element.662), channel_id=1, source_target_pairs={{0,32},{32,64},{64,96},{96,128},{128,160},{160,192},{192,224},{224... | collective-permute-start | bytes 589832 | tf_op jit(solution)/shard_map/ppermute | solution.py:35
  17.7 2.7 %collective-permute-start.7 = (f32[3,128,128]{2,1,0:T(8,128)S(1)}, f32[3,128,128]{2,1,0:T(8,128)S(1)}, u32[]{:S(2)}, u32[]{:S(2)}) collective-permute-start(f32[3,128,128]{2,1,0:T(8,128)S(1)} %get-tuple-element.658), channel_id=1, source_target_pairs={{0,32},{32,64},{64,96},{96,128},{128,160},{160,192},{192,224},{224... | collective-permute-start | bytes 589832 | tf_op jit(solution)/shard_map/ppermute | solution.py:35
  22.4 6.5 %collective-permute-done.13.refs_4_ = f32[8,8,512]{2,1,0:T(8,128)S(1)} collective-permute-done((f32[8,8,512]{2,1,0:T(8,128)S(1)}, f32[8,8,512]{2,1,0:T(8,128)S(1)}, u32[]{:S(2)}, u32[]{:S(2)}) %collective-permute-start.13) | collective-permute-done | bytes 131104 | tf_op jit(solution)/shard_map/ppermute | solution.py:35
  29.0 2.1 %collective-permute-start.15 = (f32[3,128,128]{2,1,0:T(8,128)S(1)}, f32[3,128,128]{2,1,0:T(8,128)S(1)}, u32[]{:S(2)}, u32[]{:S(2)}) collective-permute-start(f32[3,128,128]{2,1,0:T(8,128)S(1)} %get-tuple-element.668), channel_id=1, source_target_pairs={{0,32},{32,64},{64,96},{96,128},{128,160},{160,192},{192,224},{224... | collective-permute-start | bytes 589832 | tf_op jit(solution)/shard_map/ppermute | solution.py:35
  31.2 2.8 %collective-permute-start.19 = (f32[3,128,128]{2,1,0:T(8,128)S(1)}, f32[3,128,128]{2,1,0:T(8,128)S(1)}, u32[]{:S(2)}, u32[]{:S(2)}) collective-permute-start(f32[3,128,128]{2,1,0:T(8,128)S(1)} %get-tuple-element.676), channel_id=1, source_target_pairs={{0,32},{32,64},{64,96},{96,128},{128,160},{160,192},{192,224},{224... | collective-permute-start | bytes 589832 | tf_op jit(solution)/shard_map/ppermute | solution.py:35
  35.4 2.3 %collective-permute-done.16.refs_7_ = f32[3,128,128]{2,1,0:T(8,128)S(1)} collective-permute-done((f32[3,128,128]{2,1,0:T(8,128)S(1)}, f32[3,128,128]{2,1,0:T(8,128)S(1)}, u32[]{:S(2)}, u32[]{:S(2)}) %collective-permute-start.16) | collective-permute-done | bytes 196640 | tf_op jit(solution)/shard_map/ppermute | solution.py:35
  37.8 4.2 %collective-permute-start.17 = (f32[3,128,128]{2,1,0:T(8,128)S(1)}, f32[3,128,128]{2,1,0:T(8,128)S(1)}, u32[]{:S(2)}, u32[]{:S(2)}) collective-permute-start(f32[3,128,128]{2,1,0:T(8,128)S(1)} %get-tuple-element.670), channel_id=1, source_target_pairs={{0,32},{32,64},{64,96},{96,128},{128,160},{160,192},{192,224},{224... | collective-permute-start | bytes 589832 | tf_op jit(solution)/shard_map/ppermute | solution.py:35
  43.1 3.5 %collective-permute-start.21 = (f32[3,128,128]{2,1,0:T(8,128)S(1)}, f32[3,128,128]{2,1,0:T(8,128)S(1)}, u32[]{:S(2)}, u32[]{:S(2)}) collective-permute-start(f32[3,128,128]{2,1,0:T(8,128)S(1)} %get-tuple-element.678), channel_id=1, source_target_pairs={{0,32},{32,64},{64,96},{96,128},{128,160},{160,192},{192,224},{224... | collective-permute-start | bytes 589832 | tf_op jit(solution)/shard_map/ppermute | solution.py:35
  47.8 2.0 %collective-permute-done.21 = f32[3,128,128]{2,1,0:T(8,128)S(1)} collective-permute-done((f32[3,128,128]{2,1,0:T(8,128)S(1)}, f32[3,128,128]{2,1,0:T(8,128)S(1)}, u32[]{:S(2)}, u32[]{:S(2)}) %collective-permute-start.21) | collective-permute-done | bytes 196640 | tf_op jit(solution)/shard_map/ppermute | solution.py:35
  49.8 2.5 %collective-permute-done.22 = f32[3,128,128]{2,1,0:T(8,128)S(1)} collective-permute-done((f32[3,128,128]{2,1,0:T(8,128)S(1)}, f32[3,128,128]{2,1,0:T(8,128)S(1)}, u32[]{:S(2)}, u32[]{:S(2)}) %collective-permute-start.22) | collective-permute-done | bytes 196640 | tf_op jit(solution)/shard_map/ppermute | solution.py:35
  52.3 2.4 %conditional.1 = (f32[3,8,8,512]{3,2,1,0:T(8,128)}, f32[3,8,8,512]{3,2,1,0:T(8,128)}) conditional(s32[]{:T(128)} %bitcast.10, (s32[24,8,128]{2,1,0:T(8,128)S(1)}, f32[2,3,256,128]{3,2,1,0:T(8,128)S(1)}, f32[2,3,256,128]{3,2,1,0:T(8,128)S(1)}, f32[3,128,128]{2,1,0:T(8,128)S(1)}, f32[3,128,128]{2,1,0:T(8,128)S(1)}, ...), branch_computations={%region_0.0_spmd, %region_1.0_spmd, %region_2.5_spmd} | conditional | flops 393282 | bytes 12583926 | solution.py:396
  56.7 2.4 %collective-permute-start.27 = (f32[3,8,8,512]{3,2,1,0:T(8,128)}, f32[3,8,8,512]{3,2,1,0:T(8,128)S(1)}, u32[]{:S(2)}, u32[]{:S(2)}) collective-permute-start(f32[3,8,8,512]{3,2,1,0:T(8,128)} %get-tuple-element.683.refs_2_), channel_id=1, source_target_pairs={{0,1},{1,2},{2,3},{3,4},{4,5},{5,6},{6,7},{7,8},{8,9},{9,10},{10,1... | collective-permute-start | bytes 1179656 | tf_op jit(solution)/shard_map/ppermute | solution.py:35
  59.1 5.3 %collective-permute-start.24 = (f32[3,8,8,512]{3,2,1,0:T(8,128)}, f32[3,8,8,512]{3,2,1,0:T(8,128)S(1)}, u32[]{:S(2)}, u32[]{:S(2)}) collective-permute-start(f32[3,8,8,512]{3,2,1,0:T(8,128)} %get-tuple-element.680.refs_2_), channel_id=1, source_target_pairs={{1,0},{2,1},{3,2},{4,3},{5,4},{6,5},{7,6},{8,7},{9,8},{10,9},{11,1... | collective-permute-start | bytes 1179656 | tf_op jit(solution)/shard_map/ppermute | solution.py:35
  68.1 3.2 %advance.5.refs_2_ = f32[3,8,8,512]{3,2,1,0:T(8,128)S(1)} custom-call(s32[1]{0:T(128)} %bitcast.8.refs_0_, f32[3,8,8,512]{3,2,1,0:T(8,128)S(1)} %collective-permute-done.27.refs_1_, f32[3,8,8,512]{3,2,1,0:T(8,128)} %get-tuple-element.683.refs_2_, f32[3,8,8,512]{3,2,1,0:T(8,128)S(1)} %collective-permute-done.28.refs_3_, ...), custom_call_target="tpu_custom_call" | custom-call | flops 18874368 | bytes 1966080 | tf_op jit(solution)/shard_map/advance/pallas_call | solution.py:332
  71.2 4.0 %collective-permute-start.30 = (f32[3,8,8,512]{3,2,1,0:T(8,128)S(1)}, f32[3,8,8,512]{3,2,1,0:T(8,128)S(1)}, u32[]{:S(2)}, u32[]{:S(2)}) collective-permute-start(f32[3,8,8,512]{3,2,1,0:T(8,128)S(1)} %advance.5.refs_2_), channel_id=1, source_target_pairs={{1,0},{2,1},{3,2},{4,3},{5,4},{6,5},{7,6},{8,7},{9,8},{10,9},{11,1... | collective-permute-start | bytes 1179656 | tf_op jit(solution)/shard_map/ppermute | solution.py:35
  75.2 2.1 %collective-permute-start.29 = (f32[3,8,8,512]{3,2,1,0:T(8,128)S(1)}, f32[3,8,8,512]{3,2,1,0:T(8,128)S(1)}, u32[]{:S(2)}, u32[]{:S(2)}) collective-permute-start(f32[3,8,8,512]{3,2,1,0:T(8,128)S(1)} %advance.5.refs_2_), channel_id=1, source_target_pairs={{0,1},{1,2},{2,3},{3,4},{4,5},{5,6},{6,7},{7,8},{8,9},{9,10},{10,1... | collective-permute-start | bytes 1179656 | tf_op jit(solution)/shard_map/ppermute | solution.py:35
  77.4 3.2 %advance.4.refs_2_ = f32[3,8,8,512]{3,2,1,0:T(8,128)S(1)} custom-call(s32[1]{0:T(128)} %bitcast.8.refs_0_, f32[3,8,8,512]{3,2,1,0:T(8,128)S(1)} %collective-permute-done.23.refs_1_, f32[3,8,8,512]{3,2,1,0:T(8,128)} %get-tuple-element.680.refs_2_, f32[3,8,8,512]{3,2,1,0:T(8,128)S(1)} %collective-permute-done.24.refs_3_, ...), custom_call_target="tpu_custom_call" | custom-call | flops 18874368 | bytes 1966080 | tf_op jit(solution)/shard_map/advance/pallas_call | solution.py:332
  80.6 5.8 %collective-permute-start.26 = (f32[3,8,8,512]{3,2,1,0:T(8,128)S(1)}, f32[3,8,8,512]{3,2,1,0:T(8,128)S(1)}, u32[]{:S(2)}, u32[]{:S(2)}) collective-permute-start(f32[3,8,8,512]{3,2,1,0:T(8,128)S(1)} %advance.4.refs_2_), channel_id=1, source_target_pairs={{1,0},{2,1},{3,2},{4,3},{5,4},{6,5},{7,6},{8,7},{9,8},{10,9},{11,1... | collective-permute-start | bytes 1179656 | tf_op jit(solution)/shard_map/ppermute | solution.py:35
  88.3 3.2 %advance.6.refs_7_ = f32[2,3,256,128]{3,2,1,0:T(8,128)} custom-call(s32[1]{0:T(128)} %bitcast.8.refs_0_, f32[3,8,8,512]{3,2,1,0:T(8,128)S(1)} %collective-permute-done.29.refs_1_, f32[3,8,8,512]{3,2,1,0:T(8,128)S(1)} %advance.5.refs_2_, f32[3,8,8,512]{3,2,1,0:T(8,128)S(1)} %collective-permute-done.30.refs_3_, ...), custom_call_target="tpu_custom_call" | custom-call | flops 18874368 | bytes 1966080 | tf_op jit(solution)/shard_map/advance/pallas_call | solution.py:332
  91.6 5.9 %collective-permute-done.25.refs_1_ = f32[3,8,8,512]{3,2,1,0:T(8,128)S(1)} collective-permute-done((f32[3,8,8,512]{3,2,1,0:T(8,128)S(1)}, f32[3,8,8,512]{3,2,1,0:T(8,128)S(1)}, u32[]{:S(2)}, u32[]{:S(2)}) %collective-permute-start.25) | collective-permute-done | bytes 393248 | tf_op jit(solution)/shard_map/ppermute | solution.py:35
  97.5 3.2 %advance.7 = f32[2,3,256,128]{3,2,1,0:T(8,128)} custom-call(s32[1]{0:T(128)} %bitcast.8.refs_0_, f32[3,8,8,512]{3,2,1,0:T(8,128)S(1)} %collective-permute-done.25.refs_1_, f32[3,8,8,512]{3,2,1,0:T(8,128)S(1)} %advance.4.refs_2_, f32[3,8,8,512]{3,2,1,0:T(8,128)S(1)} %collective-permute-done.26.refs_3_, ...), custom_call_target="tpu_custom_call", output_to_operand_aliasing={{}: (7, {})} | custom-call | flops 18874368 | bytes 1966080 | tf_op jit(solution)/shard_map/advance/pallas_call | solution.py:332
  (53 shorter events, 21.0 us)
Async XLA Ops:
  3.4 9.1 %collective-permute-start.9 = (f32[3,128,128]{2,1,0:T(8,128)S(1)}, f32[3,128,128]{2,1,0:T(8,128)S(1)}, u32[]{:S(2)}, u32[]{:S(2)}) collective-permute-start(f32[3,128,128]{2,1,0:T(8,128)S(1)} %get-tuple-element.660), channel_id=1, source_target_pairs={{0,32},{32,64},{64,96},{96,128},{128,160},{160,192},{192,224},{224... | collective-permute-start | bytes 589832 | tf_op jit(solution)/shard_map/ppermute | solution.py:35
  5.4 8.9 %collective-permute-start.10 = (f32[3,128,128]{2,1,0:T(8,128)S(1)}, f32[3,128,128]{2,1,0:T(8,128)S(1)}, u32[]{:S(2)}, u32[]{:S(2)}) collective-permute-start(f32[3,128,128]{2,1,0:T(8,128)S(1)} %get-tuple-element.661), channel_id=1, source_target_pairs={{0,224},{32,0},{64,32},{96,64},{128,96},{160,128},{192,160},{224,1... | collective-permute-start | bytes 589832 | tf_op jit(solution)/shard_map/ppermute | solution.py:35
  5.5 12.1 %collective-permute-start.5 = (f32[3,128,128]{2,1,0:T(8,128)S(1)}, f32[3,128,128]{2,1,0:T(8,128)S(1)}, u32[]{:S(2)}, u32[]{:S(2)}) collective-permute-start(f32[3,128,128]{2,1,0:T(8,128)S(1)} %get-tuple-element.656), channel_id=1, source_target_pairs={{0,32},{32,64},{64,96},{96,128},{128,160},{160,192},{192,224},{224... | collective-permute-start | bytes 589832 | tf_op jit(solution)/shard_map/ppermute | solution.py:35
  8.6 9.0 %collective-permute-start.6 = (f32[3,128,128]{2,1,0:T(8,128)S(1)}, f32[3,128,128]{2,1,0:T(8,128)S(1)}, u32[]{:S(2)}, u32[]{:S(2)}) collective-permute-start(f32[3,128,128]{2,1,0:T(8,128)S(1)} %get-tuple-element.657), channel_id=1, source_target_pairs={{0,224},{32,0},{64,32},{96,64},{128,96},{160,128},{192,160},{224,1... | collective-permute-start | bytes 589832 | tf_op jit(solution)/shard_map/ppermute | solution.py:35
  8.8 11.7 %collective-permute-start.14 = (f32[8,8,512]{2,1,0:T(8,128)S(1)}, f32[8,8,512]{2,1,0:T(8,128)S(1)}, u32[]{:S(2)}, u32[]{:S(2)}) collective-permute-start(f32[8,8,512]{2,1,0:T(8,128)S(1)} %bitcast.40), channel_id=1, source_target_pairs={{1,0},{2,1},{3,2},{4,3},{5,4},{6,5},{7,6},{8,7},{9,8},{10,9},{11,1... | collective-permute-start | bytes 393224 | tf_op jit(solution)/shard_map/ppermute | solution.py:35
  14.3 14.5 %collective-permute-start.11 = (f32[3,128,128]{2,1,0:T(8,128)S(1)}, f32[3,128,128]{2,1,0:T(8,128)S(1)}, u32[]{:S(2)}, u32[]{:S(2)}) collective-permute-start(f32[3,128,128]{2,1,0:T(8,128)S(1)} %get-tuple-element.662), channel_id=1, source_target_pairs={{0,32},{32,64},{64,96},{96,128},{128,160},{160,192},{192,224},{224... | collective-permute-start | bytes 589832 | tf_op jit(solution)/shard_map/ppermute | solution.py:35
  17.7 11.2 %collective-permute-start.12 = (f32[3,128,128]{2,1,0:T(8,128)S(1)}, f32[3,128,128]{2,1,0:T(8,128)S(1)}, u32[]{:S(2)}, u32[]{:S(2)}) collective-permute-start(f32[3,128,128]{2,1,0:T(8,128)S(1)} %get-tuple-element.663), channel_id=1, source_target_pairs={{0,224},{32,0},{64,32},{96,64},{128,96},{160,128},{192,160},{224,1... | collective-permute-start | bytes 589832 | tf_op jit(solution)/shard_map/ppermute | solution.py:35
  17.7 11.1 %collective-permute-start.7 = (f32[3,128,128]{2,1,0:T(8,128)S(1)}, f32[3,128,128]{2,1,0:T(8,128)S(1)}, u32[]{:S(2)}, u32[]{:S(2)}) collective-permute-start(f32[3,128,128]{2,1,0:T(8,128)S(1)} %get-tuple-element.658), channel_id=1, source_target_pairs={{0,32},{32,64},{64,96},{96,128},{128,160},{160,192},{192,224},{224... | collective-permute-start | bytes 589832 | tf_op jit(solution)/shard_map/ppermute | solution.py:35
  20.5 8.4 %collective-permute-start.8 = (f32[3,128,128]{2,1,0:T(8,128)S(1)}, f32[3,128,128]{2,1,0:T(8,128)S(1)}, u32[]{:S(2)}, u32[]{:S(2)}) collective-permute-start(f32[3,128,128]{2,1,0:T(8,128)S(1)} %get-tuple-element.659), channel_id=1, source_target_pairs={{0,224},{32,0},{64,32},{96,64},{128,96},{160,128},{192,160},{224,1... | collective-permute-start | bytes 589832 | tf_op jit(solution)/shard_map/ppermute | solution.py:35
  20.5 8.4 %collective-permute-start.13 = (f32[8,8,512]{2,1,0:T(8,128)S(1)}, f32[8,8,512]{2,1,0:T(8,128)S(1)}, u32[]{:S(2)}, u32[]{:S(2)}) collective-permute-start(f32[8,8,512]{2,1,0:T(8,128)S(1)} %bitcast.41), channel_id=1, source_target_pairs={{0,1},{1,2},{2,3},{3,4},{4,5},{5,6},{6,7},{7,8},{8,9},{9,10},{10,1... | collective-permute-start | bytes 393224 | tf_op jit(solution)/shard_map/ppermute | solution.py:35
  29.0 6.4 %collective-permute-start.15 = (f32[3,128,128]{2,1,0:T(8,128)S(1)}, f32[3,128,128]{2,1,0:T(8,128)S(1)}, u32[]{:S(2)}, u32[]{:S(2)}) collective-permute-start(f32[3,128,128]{2,1,0:T(8,128)S(1)} %get-tuple-element.668), channel_id=1, source_target_pairs={{0,32},{32,64},{64,96},{96,128},{128,160},{160,192},{192,224},{224... | collective-permute-start | bytes 589832 | tf_op jit(solution)/shard_map/ppermute | solution.py:35
  31.1 6.6 %collective-permute-start.16 = (f32[3,128,128]{2,1,0:T(8,128)S(1)}, f32[3,128,128]{2,1,0:T(8,128)S(1)}, u32[]{:S(2)}, u32[]{:S(2)}) collective-permute-start(f32[3,128,128]{2,1,0:T(8,128)S(1)} %get-tuple-element.669), channel_id=1, source_target_pairs={{0,224},{32,0},{64,32},{96,64},{128,96},{160,128},{192,160},{224,1... | collective-permute-start | bytes 589832 | tf_op jit(solution)/shard_map/ppermute | solution.py:35
  31.2 10.8 %collective-permute-start.19 = (f32[3,128,128]{2,1,0:T(8,128)S(1)}, f32[3,128,128]{2,1,0:T(8,128)S(1)}, u32[]{:S(2)}, u32[]{:S(2)}) collective-permute-start(f32[3,128,128]{2,1,0:T(8,128)S(1)} %get-tuple-element.676), channel_id=1, source_target_pairs={{0,32},{32,64},{64,96},{96,128},{128,160},{160,192},{192,224},{224... | collective-permute-start | bytes 589832 | tf_op jit(solution)/shard_map/ppermute | solution.py:35
  34.0 9.0 %collective-permute-start.20 = (f32[3,128,128]{2,1,0:T(8,128)S(1)}, f32[3,128,128]{2,1,0:T(8,128)S(1)}, u32[]{:S(2)}, u32[]{:S(2)}) collective-permute-start(f32[3,128,128]{2,1,0:T(8,128)S(1)} %get-tuple-element.677), channel_id=1, source_target_pairs={{0,224},{32,0},{64,32},{96,64},{128,96},{160,128},{192,160},{224,1... | collective-permute-start | bytes 589832 | tf_op jit(solution)/shard_map/ppermute | solution.py:35
  37.8 10.0 %collective-permute-start.17 = (f32[3,128,128]{2,1,0:T(8,128)S(1)}, f32[3,128,128]{2,1,0:T(8,128)S(1)}, u32[]{:S(2)}, u32[]{:S(2)}) collective-permute-start(f32[3,128,128]{2,1,0:T(8,128)S(1)} %get-tuple-element.670), channel_id=1, source_target_pairs={{0,32},{32,64},{64,96},{96,128},{128,160},{160,192},{192,224},{224... | collective-permute-start | bytes 589832 | tf_op jit(solution)/shard_map/ppermute | solution.py:35
  43.1 6.7 %collective-permute-start.21 = (f32[3,128,128]{2,1,0:T(8,128)S(1)}, f32[3,128,128]{2,1,0:T(8,128)S(1)}, u32[]{:S(2)}, u32[]{:S(2)}) collective-permute-start(f32[3,128,128]{2,1,0:T(8,128)S(1)} %get-tuple-element.678), channel_id=1, source_target_pairs={{0,32},{32,64},{64,96},{96,128},{128,160},{160,192},{192,224},{224... | collective-permute-start | bytes 589832 | tf_op jit(solution)/shard_map/ppermute | solution.py:35
  54.7 11.5 %collective-permute-start.28 = (f32[3,8,8,512]{3,2,1,0:T(8,128)}, f32[3,8,8,512]{3,2,1,0:T(8,128)S(1)}, u32[]{:S(2)}, u32[]{:S(2)}) collective-permute-start(f32[3,8,8,512]{3,2,1,0:T(8,128)} %get-tuple-element.683.refs_2_), channel_id=1, source_target_pairs={{1,0},{2,1},{3,2},{4,3},{5,4},{6,5},{7,6},{8,7},{9,8},{10,9},{11,1... | collective-permute-start | bytes 1179656 | tf_op jit(solution)/shard_map/ppermute | solution.py:35
  56.7 11.4 %collective-permute-start.27 = (f32[3,8,8,512]{3,2,1,0:T(8,128)}, f32[3,8,8,512]{3,2,1,0:T(8,128)S(1)}, u32[]{:S(2)}, u32[]{:S(2)}) collective-permute-start(f32[3,8,8,512]{3,2,1,0:T(8,128)} %get-tuple-element.683.refs_2_), channel_id=1, source_target_pairs={{0,1},{1,2},{2,3},{3,4},{4,5},{5,6},{6,7},{7,8},{8,9},{9,10},{10,1... | collective-permute-start | bytes 1179656 | tf_op jit(solution)/shard_map/ppermute | solution.py:35
  59.1 18.3 %collective-permute-start.24 = (f32[3,8,8,512]{3,2,1,0:T(8,128)}, f32[3,8,8,512]{3,2,1,0:T(8,128)S(1)}, u32[]{:S(2)}, u32[]{:S(2)}) collective-permute-start(f32[3,8,8,512]{3,2,1,0:T(8,128)} %get-tuple-element.680.refs_2_), channel_id=1, source_target_pairs={{1,0},{2,1},{3,2},{4,3},{5,4},{6,5},{7,6},{8,7},{9,8},{10,9},{11,1... | collective-permute-start | bytes 1179656 | tf_op jit(solution)/shard_map/ppermute | solution.py:35
  64.3 13.0 %collective-permute-start.23 = (f32[3,8,8,512]{3,2,1,0:T(8,128)}, f32[3,8,8,512]{3,2,1,0:T(8,128)S(1)}, u32[]{:S(2)}, u32[]{:S(2)}) collective-permute-start(f32[3,8,8,512]{3,2,1,0:T(8,128)} %get-tuple-element.680.refs_2_), channel_id=1, source_target_pairs={{0,1},{1,2},{2,3},{3,4},{4,5},{5,6},{6,7},{7,8},{8,9},{9,10},{10,1... | collective-permute-start | bytes 1179656 | tf_op jit(solution)/shard_map/ppermute | solution.py:35
  71.2 17.0 %collective-permute-start.30 = (f32[3,8,8,512]{3,2,1,0:T(8,128)S(1)}, f32[3,8,8,512]{3,2,1,0:T(8,128)S(1)}, u32[]{:S(2)}, u32[]{:S(2)}) collective-permute-start(f32[3,8,8,512]{3,2,1,0:T(8,128)S(1)} %advance.5.refs_2_), channel_id=1, source_target_pairs={{1,0},{2,1},{3,2},{4,3},{5,4},{6,5},{7,6},{8,7},{9,8},{10,9},{11,1... | collective-permute-start | bytes 1179656 | tf_op jit(solution)/shard_map/ppermute | solution.py:35
  75.2 13.0 %collective-permute-start.29 = (f32[3,8,8,512]{3,2,1,0:T(8,128)S(1)}, f32[3,8,8,512]{3,2,1,0:T(8,128)S(1)}, u32[]{:S(2)}, u32[]{:S(2)}) collective-permute-start(f32[3,8,8,512]{3,2,1,0:T(8,128)S(1)} %advance.5.refs_2_), channel_id=1, source_target_pairs={{0,1},{1,2},{2,3},{3,4},{4,5},{5,6},{6,7},{7,8},{8,9},{9,10},{10,1... | collective-permute-start | bytes 1179656 | tf_op jit(solution)/shard_map/ppermute | solution.py:35
  80.6 11.0 %collective-permute-start.26 = (f32[3,8,8,512]{3,2,1,0:T(8,128)S(1)}, f32[3,8,8,512]{3,2,1,0:T(8,128)S(1)}, u32[]{:S(2)}, u32[]{:S(2)}) collective-permute-start(f32[3,8,8,512]{3,2,1,0:T(8,128)S(1)} %advance.4.refs_2_), channel_id=1, source_target_pairs={{1,0},{2,1},{3,2},{4,3},{5,4},{6,5},{7,6},{8,7},{9,8},{10,9},{11,1... | collective-permute-start | bytes 1179656 | tf_op jit(solution)/shard_map/ppermute | solution.py:35
  86.3 11.2 %collective-permute-start.25 = (f32[3,8,8,512]{3,2,1,0:T(8,128)S(1)}, f32[3,8,8,512]{3,2,1,0:T(8,128)S(1)}, u32[]{:S(2)}, u32[]{:S(2)}) collective-permute-start(f32[3,8,8,512]{3,2,1,0:T(8,128)S(1)} %advance.4.refs_2_), channel_id=1, source_target_pairs={{0,1},{1,2},{2,3},{3,4},{4,5},{5,6},{6,7},{7,8},{8,9},{9,10},{10,1... | collective-permute-start | bytes 1179656 | tf_op jit(solution)/shard_map/ppermute | solution.py:35
  (5 other events, 25.7 us)
where the time goes:
time: 101 us
  starting transfers between devices  54.7 us (54%)
  waiting for transfers between devices  25.2 us (25%)
  Pallas kernels  17.6 us (17%)
  local copies, waits for them, and re-layouts  2.31 us (2%)
    ppermute x26, starting transfers between devices, neighbour(): return lax.ppermute(value, axis, pairs)  54.7 us
    ppermute x26, waiting for transfers between devices, neighbour(): return lax.ppermute(value, axis, pairs)  25.2 us
    pallas_call x4, Pallas kernels, advance(): pl.pallas_call(kernel, grid=(1,), out_shape=jax.ShapeDtypeStruct(out_shap...  12.7 us
    pallas_call x2, Pallas kernels, collect(): pl.pallas_call(lambda *refs: collect_kernel(per, rows, entry, len(chains)...  2.44 us
  transfers between devices with their start and end apart: 26, of which 10 were waited for; matrix products, arithmetic and copies ran while one was open for 1% of the time, Pallas kernels for 10%

commit v1 on v0

--- a/solution.py
+++ b/solution.py
@@ -51,43 +51,69 @@
     return value
 
 
-def plan_kernel(devices, per, rounds, me_ref, parents_ref, table_ref, case_ref):
+def sent_row(per, round_index, direction):
+    return 2 * per + 4 * round_index + 2 * direction
+
+
+def plan_kernel(devices, per, rounds, me_ref, parents_hbm, own_hbm, table_ref, case_ref, own_ref, parents_ref, sems):
+    named = pltpu.make_async_copy(parents_hbm, parents_ref, sems.at[0])
+    fetched = pltpu.make_async_copy(own_hbm, own_ref, sems.at[1])
+    named.start()
+    fetched.start()
     count = devices * per
     pairs = 2 * count
     half = devices // 2
     me = me_ref[0]
+    slot = lax.broadcasted_iota(jnp.int32, (SUBLANES, LANES), 1)
+    item = lax.rem(slot, count)
+    direction = slot // count
+    origin = item // per
+    sibling = item + 1 - 2 * lax.rem(item, 2)
+    zero = jnp.zeros((SUBLANES, LANES), jnp.int32)
+    reach, opposite, other_opposite, other_up, other_down = zero, zero, zero, zero, zero
+    named.wait()
+    for entry in range(count):
+        parent = parents_ref[entry]
+        hops = lax.rem(entry // per - parent // per + devices, devices)
+        up = jnp.where(hops < half, hops, 0)
+        down = jnp.where(hops > half, devices - hops, 0)
+        tie = jnp.where(hops == half, 1, 0)
+        mine, other = item == parent, sibling == parent
+        reach = jnp.maximum(reach, jnp.where(mine, jnp.where(direction == 0, up, down), 0))
+        opposite = jnp.maximum(opposite, jnp.where(mine, tie, 0))
+        other_opposite = jnp.maximum(other_opposite, jnp.where(other, tie, 0))
+        other_up = jnp.maximum(other_up, jnp.where(other, up, 0))
+        other_down = jnp.maximum(other_down, jnp.where(other, down, 0))
+    goes_down = jnp.where(
+        other_opposite > 0,
+        lax.rem(origin + item, 2),
+        jnp.where(other_up == other_down, lax.rem(origin, 2), jnp.where(other_up < other_down, 0, 1)),
+    )
+    reach = jnp.where((opposite > 0) & (goes_down == direction), half, reach)
+
     down_row = lax.broadcasted_iota(jnp.int32, (pairs, LANES), 0)
     along_row = lax.broadcasted_iota(jnp.int32, (pairs, LANES), 1)
 
     def facts(index):
-        item = lax.rem(index, count)
-        return index // count, item, item // per
+        thing = lax.rem(index, count)
+        return index // count, thing, thing // per
 
     sides = [facts(index) for index in (down_row, along_row)]
-    far = [jnp.zeros((pairs, LANES), jnp.int32) for _ in range(2)]
-    for entry in range(count):
-        parent = parents_ref[entry]
-        origin = parent // per
-        hops = lax.rem(entry // per - origin + devices, devices)
-        goes_up = jnp.logical_or(hops < half, jnp.logical_and(hops == half, lax.rem(origin, 2) == 0))
-        slot = parent + jnp.where(goes_up, 0, count)
-        distance = jnp.where(goes_up, hops, devices - hops)
-        far = [jnp.maximum(f, jnp.where(index == slot, distance, 0)) for f, index in zip(far, (down_row, along_row))]
+    far_along = jnp.broadcast_to(reach[:1], (pairs, LANES))
+    far_down = jnp.max(jnp.where(down_row == along_row, far_along, 0), axis=1, keepdims=True)
+    far = [jnp.broadcast_to(far_down, (pairs, LANES)), far_along]
 
     def put(row, value):
         table_ref[row] = jnp.broadcast_to(value, (SUBLANES, LANES)).astype(jnp.int32)
 
-    for k in range(per):
-        put(k, jnp.full((SUBLANES, LANES), me * per + k, jnp.int32))
-        put(per + k, jnp.full((SUBLANES, LANES), parents_ref[me * per + k], jnp.int32))
     position = [jnp.zeros((pairs, LANES), jnp.int32) for _ in range(2)]
     unmet = []
     for r in range(rounds):
         left, link, key = [], [], []
-        for (direction, item, origin), f, p, index in zip(sides, far, position, (down_row, along_row)):
-            step = jnp.where(direction == 0, p, devices - p)
+        for (way, _, start), f, p, index in zip(sides, far, position, (down_row, along_row)):
+            step = jnp.where(way == 0, p, devices - p)
             left.append(f - p)
-            link.append(lax.rem(origin + step, devices) + direction * devices)
+            link.append(lax.rem(start + step, devices) + way * devices)
             key.append(jnp.where(f > p, (f - p) * pairs + pairs - 1 - index, -1))
         same = link[0] == link[1]
         beaten_down = jnp.max(jnp.where(same & (key[1] > key[0]), 1, 0), axis=1, keepdims=True)
@@ -96,28 +122,38 @@
             jnp.where((left[0] > 0) & (jnp.broadcast_to(beaten_down, left[0].shape) == 0), 1, 0),
             jnp.where((left[1] > 0) & (jnp.broadcast_to(beaten_along, left[1].shape) == 0), 1, 0),
         ]
-        for q, (place, direction) in enumerate(((me, 0), (me + devices - 1, 0), (me, 1), (me + 1, 1))):
-            here = (wins[1] > 0) & (link[1] == lax.rem(place, devices) + direction * devices)
+        for q, (place, way) in enumerate(((me, 0), (me + devices - 1, 0), (me, 1), (me + 1, 1))):
+            here = (wins[1] > 0) & (link[1] == lax.rem(place, devices) + way * devices)
             put(2 * per + 4 * r + q, jnp.max(jnp.where(here, sides[1][1], -1)[:SUBLANES], axis=1, keepdims=True))
         position = [p + w for p, w in zip(position, wins)]
         unmet.append(jnp.max(jnp.where(far[1] > position[1], 1, 0)[:SUBLANES], axis=1, keepdims=True))
-    case_ref[...] = jnp.broadcast_to(unmet[-2] + unmet[-1], (SUBLANES, LANES))
-
-
-def plan(parents, me, devices, per, rounds):
-    smem = pl.BlockSpec(memory_space=pltpu.SMEM)
+    case = jnp.broadcast_to(unmet[-2] + unmet[-1], (SUBLANES, LANES))
+    case_ref[...] = case
+    for k in range(per):
+        put(k, jnp.full((SUBLANES, LANES), me * per + k, jnp.int32))
+        entry = jnp.full((SUBLANES, LANES), parents_ref[me * per + k], jnp.int32)
+        put(per + k, jnp.where(case == 2, count + k, entry))
+        last = sent_row(per, rounds - 1, k) + 1
+        table_ref[last] = jnp.where(case == 2, count + k, table_ref[last])
+    fetched.wait()
+
+
+def plan(parents, own, me, devices, per, rounds):
     vmem = pl.BlockSpec(memory_space=pltpu.VMEM)
+    hbm = pl.BlockSpec(memory_space=pltpu.HBM)
     return pl.pallas_call(
         lambda *refs: plan_kernel(devices, per, rounds, *refs),
         out_shape=(
             jax.ShapeDtypeStruct((2 * per + 4 * rounds, SUBLANES, LANES), jnp.int32),
             jax.ShapeDtypeStruct((SUBLANES, LANES), jnp.int32),
+            jax.ShapeDtypeStruct(own.shape, own.dtype),
         ),
-        in_specs=[smem, smem],
-        out_specs=(vmem, vmem),
+        in_specs=[pl.BlockSpec(memory_space=pltpu.SMEM), hbm, hbm],
+        out_specs=(vmem, vmem, vmem),
+        scratch_shapes=[pltpu.SMEM(parents.shape, jnp.int32), pltpu.SemaphoreType.DMA((2,))],
         compiler_params=pltpu.CompilerParams(vmem_limit_bytes=VMEM_LIMIT),
         name="plan",
-    )(me, parents)
+    )(me, parents, own)
 
 
 def candidates_of(per, own_ref, received, field, base, rows):
@@ -125,29 +161,28 @@
     return values + [ref[field].reshape(-1, SUBLANES, LANES) for ref in received]
 
 
-def select_kernel(per, base, round_index, table_ref, own_ref, *refs):
-    received, (up_ref, down_ref) = refs[:-2], refs[-2:]
-    fields, rows, _ = up_ref.shape
-    names = identity_rows(per, len(received))
+def received_rows(per, direction, received):
+    return [sent_row(per, r, direction) + 1 for r in range(received)]
+
+
+def select_kernel(per, base, direction, table_ref, own_ref, *refs):
+    received, out_ref = refs[:-1], refs[-1]
+    fields, rows, _ = out_ref.shape
+    names = list(range(per)) + received_rows(per, direction, len(received))
     for f in range(fields):
         values = candidates_of(per, own_ref, received, f, base, rows)
-        for out_ref, q in ((up_ref, 0), (down_ref, 2)):
-            out_ref[f] = choose(table_ref, 2 * per + 4 * round_index + q, names, values).reshape(rows, LANES)
-
-
-def identity_rows(per, received):
-    return list(range(per)) + [2 * per + 4 * (k // 2) + (1, 3)[k % 2] for k in range(received)]
-
-
-def select(table, own, received, base, rows, round_index):
+        wanted = sent_row(per, len(received), direction)
+        out_ref[f] = choose(table_ref, wanted, names, values).reshape(rows, LANES)
+
+
+def select(table, own, received, base, rows, direction):
     per, fields = own.shape[:2]
     vmem = pl.BlockSpec(memory_space=pltpu.VMEM)
-    shape = jax.ShapeDtypeStruct((fields, rows, LANES), jnp.float32)
     return pl.pallas_call(
-        lambda *refs: select_kernel(per, base, round_index, *refs),
-        out_shape=(shape, shape),
+        lambda *refs: select_kernel(per, base, direction, *refs),
+        out_shape=jax.ShapeDtypeStruct((fields, rows, LANES), jnp.float32),
         in_specs=[vmem] * (2 + len(received)),
-        out_specs=(vmem, vmem),
+        out_specs=vmem,
         cost_estimate=pl.CostEstimate(flops=0, bytes_accessed=4 * fields * rows * LANES * 4, transcendentals=0),
         compiler_params=pltpu.CompilerParams(vmem_limit_bytes=VMEM_LIMIT),
         name="select",
@@ -167,52 +202,42 @@
     lax.fori_loop(0, rows, one_row, 0)
 
 
-def collect_kernel(per, rows, entry, chains, table_ref, own_ref, noise_ref, *refs):
+def collect_kernel(per, rows, entry, chains, with_depth, table_ref, own_ref, noise_ref, *refs):
     out_ref, value_ref = refs[-2:]
     received = refs[:-2]
-    each = len(received) // chains
-    fields, count, _ = value_ref.shape
-    part = count // chains
-    names = identity_rows(per, each)
+    if with_depth:
+        depth_ref, received = received[0], received[1:]
+        value_ref[value_ref.shape[0] - 1] = depth_ref[...]
+    each = len(received) // (2 * chains)
+    fields = own_ref.shape[1]
+    part = value_ref.shape[1] // chains
+    names = list(range(per)) + received_rows(per, 0, each) + received_rows(per, 1, each)
     for f in range(fields):
         for h in range(chains):
-            values = candidates_of(per, own_ref, received[h * each:(h + 1) * each], f, h * part, part)
-            found = choose(table_ref, per + entry, names, values).reshape(part, LANES)
+            pieces = received[2 * h * each:2 * (h + 1) * each]
+            found = choose(table_ref, per + entry, names, candidates_of(per, own_ref, pieces, f, h * part, part))
             where = pl.ds(h * part, part)
-            value_ref[f, where, :] = found + noise_ref[entry, f, where, :]
+            value_ref[f, where, :] = found.reshape(part, LANES) + noise_ref[entry, f, where, :]
     spread(rows, value_ref, out_ref)
 
 
-def collect(table, own, noise, chains, rows, entry):
+def collect(table, own, noise, chains, rows, entry, depth=None):
     per, fields, count, _ = own.shape
     lon = count // rows * LANES
+    planes = fields + (depth is not None)
     vmem = pl.BlockSpec(memory_space=pltpu.VMEM)
-    pieces = [piece for chain in chains for piece in chain]
+    operands = [table, own, noise] + ([] if depth is None else [depth])
+    operands += [piece for chain in chains for stream in chain for piece in stream]
     return pl.pallas_call(
-        lambda *refs: collect_kernel(per, rows, entry, len(chains), *refs),
-        out_shape=jax.ShapeDtypeStruct((fields, rows, SUBLANES, lon // SUBLANES), jnp.float32),
-        in_specs=[vmem] * (3 + len(pieces)),
+        lambda *refs: collect_kernel(per, rows, entry, len(chains), depth is not None, *refs),
+        out_shape=jax.ShapeDtypeStruct((planes, rows, SUBLANES, lon // SUBLANES), jnp.float32),
+        in_specs=[vmem] * len(operands),
         out_specs=vmem,
-        scratch_shapes=[pltpu.VMEM((fields, count, LANES), jnp.float32)],
+        scratch_shapes=[pltpu.VMEM((planes, count, LANES), jnp.float32)],
         cost_estimate=pl.CostEstimate(flops=fields * rows * lon, bytes_accessed=12 * fields * rows * lon, transcendentals=0),
         compiler_params=pltpu.CompilerParams(vmem_limit_bytes=VMEM_LIMIT),
         name="collect",
-    )(table, own, noise, *pieces)
-
-
-def unpack_rows(rows, source):
-    fields, count, _ = source.shape
-    lon = count // rows * LANES
-    vmem = pl.BlockSpec(memory_space=pltpu.VMEM)
-    return pl.pallas_call(
-        lambda *refs: spread(rows, *refs),
-        out_shape=jax.ShapeDtypeStruct((fields, rows, SUBLANES, lon // SUBLANES), jnp.float32),
-        in_specs=[vmem],
-        out_specs=vmem,
-        cost_estimate=pl.CostEstimate(flops=0, bytes_accessed=8 * fields * rows * lon, transcendentals=0),
-        compiler_params=pltpu.CompilerParams(vmem_limit_bytes=VMEM_LIMIT),
-        name="unpack",
-    )(source)
+    )(*operands)
 
 
 def advance_kernel(rows, total_rows, final, place_ref, before, own, after, d_before, d_own, d_after, out_ref, state, first, second, third, depth):
@@ -238,8 +263,8 @@
         ]
 
     for block, (strip, d) in enumerate(((before, d_before), (own, d_own), (after, d_after))):
-        state[:, block * rows:(block + 1) * rows] = strip[...]
-        depth[block * rows:(block + 1) * rows] = d[...]
+        state[:, block * rows:(block + 1) * rows] = strip[:state.shape[0]]
+        depth[block * rows:(block + 1) * rows] = d[state.shape[0]]
 
     def stage(source, low, high, emit):
         def flux(r):
@@ -306,7 +331,8 @@
 
 
 def advance(strips, depth_strips, place, total_rows, final=None):
-    fields, rows, _, width = strips[0].shape
+    _, rows, _, width = strips[0].shape
+    fields = depth_strips[0].shape[0] - 1
     reach_rows = 2 * REACH + rows
     plane = pltpu.VMEM((fields, reach_rows, SUBLANES, width), jnp.float32)
     vmem = pl.BlockSpec(memory_space=pltpu.VMEM)
@@ -315,7 +341,7 @@
     in_specs = [smem] + [vmem] * 6
     options = {}
     if final is None:
-        out_shape, out_specs = strips[0].shape, vmem
+        out_shape, out_specs = (fields, *strips[0].shape[1:]), vmem
     else:
         member, members, partial = final
         count = rows * SUBLANES * width // LANES
@@ -351,31 +377,30 @@
     devices = lax.axis_size("dom")
     me = lax.axis_index("dom").astype(jnp.int32)
     place = lax.axis_index("lat").astype(jnp.int32)[None]
-    table, case = plan(parents, me[None], devices, per, ROUNDS + 1)
-    tiles = to_tiles(ensemble)
+    table, case, tiles = plan(parents, to_tiles(ensemble), me[None], devices, per, ROUNDS + 1)
     noise = to_tiles(perturbation)
     count = tiles.shape[2]
     part = count // CHAINS
 
-    def exchange(chains, round_index):
-        sends = [select(table, tiles, chain, h * part, part, round_index) for h, chain in enumerate(chains)]
+    def fresh(chains):
         return [
-            chain + [neighbour(up, "dom", 1, True), neighbour(down, "dom", -1, True)]
-            for chain, (up, down) in zip(chains, sends)
+            [
+                neighbour(select(table, tiles, stream, h * part, part, direction), "dom", 1 - 2 * direction, True)
+                for direction, stream in enumerate(chain)
+            ]
+            for h, chain in enumerate(chains)
         ]
 
-    depth_rows = unpack_rows(rows, to_tiles(depth)[None])[0]
-    depth_before, depth_after = both_sides(depth_rows)
-
-    chains = [[] for _ in range(CHAINS)]
-    for round_index in range(ROUNDS):
-        chains = exchange(chains, round_index)
-        if round_index == 1:
-            chains, depth_before, depth_after = lax.optimization_barrier((chains, depth_before, depth_after))
-    depth_strips = (depth_before, depth_rows, depth_after)
+    def extend(chains, pieces):
+        return [[stream + [piece] for stream, piece in zip(*pair)] for pair in zip(chains, pieces)]
+
+    chains = [[[], []] for _ in range(CHAINS)]
+    for _ in range(ROUNDS):
+        chains = extend(chains, fresh(chains))
 
     def gather(chains):
-        return tuple(collect(table, tiles, noise, chains, rows, k) for k in range(per))
+        depth_tiles = to_tiles(depth)
+        return [collect(table, tiles, noise, chains, rows, k, depth_tiles if k == 0 else None) for k in range(per)]
 
     def all_round(chains):
         own_parents = lax.dynamic_slice_in_dim(parents, me * per, per, 0)
@@ -391,17 +416,21 @@
 
         start = tuple(tiles[own_parents[e] % per] for e in range(per))
         found = lax.fori_loop(0, devices - 1, turn, (tiles, start))[1]
-        return tuple(unpack_rows(rows, found[k] + noise[k]) for k in range(per))
+        return [[entry[:, h * part:(h + 1) * part] for entry in found] for h in range(CHAINS)]
 
     states = lax.switch(
-        case[0, 0], [gather, lambda chains: gather(exchange(chains, ROUNDS)), all_round], chains
+        case[0, 0],
+        [gather, lambda chains: gather(extend(chains, fresh(chains))), lambda chains: gather(extend(chains, all_round(chains)))],
+        chains,
     )
+    depth_strips = None
     for _ in range(STEPS // STEPS_PER_EXCHANGE - 1):
-        sides = [both_sides(state) for state in states]
-        states = [
-            advance((before, state, after), depth_strips, place, total_rows)
-            for state, (before, after) in zip(states, sides)
-        ]
+        strips = []
+        for state in states:
+            before, after = both_sides(state)
+            strips.append((before, state, after))
+        depth_strips = depth_strips or strips[0]
+        states = [advance(strip, depth_strips, place, total_rows) for strip in strips]
     result = None
     for member, state in enumerate(states):
         before, after = both_sides(state)

time: 101 us -> 101 us (level); the launches traced: 101 us -> 98.6 us
  Pallas kernels: 17.6 us -> 25.4 us
  starting transfers between devices: 54.7 us -> 48.2 us
  waiting for transfers between devices: 25.2 us -> 21.8 us
    ppermute x26 -> x24, starting transfers between devices: 54.7 us -> 48.2 us  [neighbour(): return lax.ppermute(value, axis, pairs)]
    ppermute x26 -> x24, waiting for transfers between devices: 25.2 us -> 21.8 us  [neighbour(): return lax.ppermute(value, axis, pairs)]
    pallas_call x2, Pallas kernels: 2.44 us -> 5.4 us  [collect(): pl.pallas_call(lambda *refs: collect_kernel(per, rows, entry, len(chains)...]
    pallas_call x9 -> x16, Pallas kernels: 0.81 us -> 3.32 us  [select(): pl.pallas_call(lambda *refs: select_kernel(per, base, direction, *refs),...]
    pallas_call x4, Pallas kernels: 12.7 us -> 14.9 us  [advance(): pl.pallas_call(kernel, grid=(1,), out_shape=jax.ShapeDtypeStruct(out_shap...]
  transfers between devices with their start and end apart: 26 -> 24, of which waited for: 10 -> 14; matrix products, arithmetic and copies ran while one was open for 1% -> 1% of each run, Pallas kernels for 10% -> 14%
where the time goes in v1:
time: 101 us; the launch traced here: 98.6 us
  starting transfers between devices  48.2 us (48%)
  Pallas kernels  25.4 us (25%)
  waiting for transfers between devices  21.8 us (22%)
  local copies, waits for them, and re-layouts  2.31 us (2%)
    ppermute x24, starting transfers between devices, neighbour(): return lax.ppermute(value, axis, pairs)  48.2 us
    ppermute x24, waiting for transfers between devices, neighbour(): return lax.ppermute(value, axis, pairs)  21.8 us
    pallas_call x4, Pallas kernels, advance(): pl.pallas_call(kernel, grid=(1,), out_shape=jax.ShapeDtypeStruct(out_shap...  14.9 us
    pallas_call x2, Pallas kernels, collect(): pl.pallas_call(lambda *refs: collect_kernel(per, rows, entry, len(chains)...  5.4 us
    pallas_call x16, Pallas kernels, select(): pl.pallas_call(lambda *refs: select_kernel(per, base, direction, *refs),...  3.32 us
  transfers between devices with their start and end apart: 24, of which 14 were waited for; matrix products, arithmetic and copies ran while one was open for 1% of the time, Pallas kernels for 14%

profile of v1, /device:TPU:88, one launch (start us, length us, event | category | flops | bytes accessed | tf_op | source)
XLA Modules:
  0.0 98.6 jit_solution(2130860415451624563)
XLA Ops:
  5.8 3.1 %collective-permute-start.13 = (f32[3,128,128]{2,1,0:T(8,128)S(1)}, f32[3,128,128]{2,1,0:T(8,128)S(1)}, u32[]{:S(2)}, u32[]{:S(2)}) collective-permute-start(f32[3,128,128]{2,1,0:T(8,128)S(1)} %select.82), channel_id=1, source_target_pairs={{0,32},{32,64},{64,96},{96,128},{128,160},{160,192},{192,224},{224... | collective-permute-start | bytes 589832 | tf_op jit(solution)/shard_map/ppermute | solution.py:35
  9.0 2.4 %collective-permute-done.5.refs_2_ = f32[3,128,128]{2,1,0:T(8,128)S(1)} collective-permute-done((f32[3,128,128]{2,1,0:T(8,128)S(1)}, f32[3,128,128]{2,1,0:T(8,128)S(1)}, u32[]{:S(2)}, u32[]{:S(2)}) %collective-permute-start.5) | collective-permute-done | bytes 196640 | tf_op jit(solution)/shard_map/ppermute | solution.py:35
  11.4 2.6 %collective-permute-start.6 = (f32[3,128,128]{2,1,0:T(8,128)S(1)}, f32[3,128,128]{2,1,0:T(8,128)S(1)}, u32[]{:S(2)}, u32[]{:S(2)}) collective-permute-start(f32[3,128,128]{2,1,0:T(8,128)S(1)} %select.75), channel_id=1, source_target_pairs={{0,32},{32,64},{64,96},{96,128},{128,160},{160,192},{192,224},{224... | collective-permute-start | bytes 589832 | tf_op jit(solution)/shard_map/ppermute | solution.py:35
  15.7 2.6 %collective-permute-start.14 = (f32[3,128,128]{2,1,0:T(8,128)S(1)}, f32[3,128,128]{2,1,0:T(8,128)S(1)}, u32[]{:S(2)}, u32[]{:S(2)}) collective-permute-start(f32[3,128,128]{2,1,0:T(8,128)S(1)} %select.83), channel_id=1, source_target_pairs={{0,32},{32,64},{64,96},{96,128},{128,160},{160,192},{192,224},{224... | collective-permute-start | bytes 589832 | tf_op jit(solution)/shard_map/ppermute | solution.py:35
  19.9 2.8 %collective-permute-start.7 = (f32[3,128,128]{2,1,0:T(8,128)S(1)}, f32[3,128,128]{2,1,0:T(8,128)S(1)}, u32[]{:S(2)}, u32[]{:S(2)}) collective-permute-start(f32[3,128,128]{2,1,0:T(8,128)S(1)} %select.76), channel_id=1, source_target_pairs={{0,32},{32,64},{64,96},{96,128},{128,160},{160,192},{192,224},{224... | collective-permute-start | bytes 589832 | tf_op jit(solution)/shard_map/ppermute | solution.py:35
  24.1 3.3 %collective-permute-start.15 = (f32[3,128,128]{2,1,0:T(8,128)S(1)}, f32[3,128,128]{2,1,0:T(8,128)}, u32[]{:S(2)}, u32[]{:S(2)}) collective-permute-start(f32[3,128,128]{2,1,0:T(8,128)S(1)} %select.84), channel_id=1, source_target_pairs={{0,32},{32,64},{64,96},{96,128},{128,160},{160,192},{192,224},{224... | collective-permute-start | bytes 589832 | tf_op jit(solution)/shard_map/ppermute | solution.py:35
  28.3 3.5 %collective-permute-start.8 = (f32[3,128,128]{2,1,0:T(8,128)S(1)}, f32[3,128,128]{2,1,0:T(8,128)}, u32[]{:S(2)}, u32[]{:S(2)}) collective-permute-start(f32[3,128,128]{2,1,0:T(8,128)S(1)} %select.77), channel_id=1, source_target_pairs={{0,32},{32,64},{64,96},{96,128},{128,160},{160,192},{192,224},{224... | collective-permute-start | bytes 589832 | tf_op jit(solution)/shard_map/ppermute | solution.py:35
  34.4 3.5 %collective-permute-start.16 = (f32[3,128,128]{2,1,0:T(8,128)S(1)}, f32[3,128,128]{2,1,0:T(8,128)}, u32[]{:S(2)}, u32[]{:S(2)}) collective-permute-start(f32[3,128,128]{2,1,0:T(8,128)S(1)} %select.85), channel_id=1, source_target_pairs={{0,32},{32,64},{64,96},{96,128},{128,160},{160,192},{192,224},{224... | collective-permute-start | bytes 589832 | tf_op jit(solution)/shard_map/ppermute | solution.py:35
  40.1 2.2 %collective-permute-done.12 = f32[3,128,128]{2,1,0:T(8,128)} collective-permute-done((f32[3,128,128]{2,1,0:T(8,128)S(1)}, f32[3,128,128]{2,1,0:T(8,128)}, u32[]{:S(2)}, u32[]{:S(2)}) %collective-permute-start.12) | collective-permute-done | bytes 196640 | tf_op jit(solution)/shard_map/ppermute | solution.py:35
  42.3 3.6 %collective-permute-done.20 = f32[3,128,128]{2,1,0:T(8,128)} collective-permute-done((f32[3,128,128]{2,1,0:T(8,128)S(1)}, f32[3,128,128]{2,1,0:T(8,128)}, u32[]{:S(2)}, u32[]{:S(2)}) %collective-permute-start.20) | collective-permute-done | bytes 196640 | tf_op jit(solution)/shard_map/ppermute | solution.py:35
  45.9 5.4 %conditional.1 = (f32[4,8,8,512]{3,2,1,0:T(8,128)}, f32[3,8,8,512]{3,2,1,0:T(8,128)}) conditional(s32[]{:T(128)} %bitcast.26, (f32[8,4096]{1,0:T(8,128)}, s32[24,8,128]{2,1,0:T(8,128)S(1)}, f32[2,3,256,128]{3,2,1,0:T(8,128)S(1)}, f32[2,3,256,128]{3,2,1,0:T(8,128)S(1)}, f32[3,128,128]{2,1,0:T(8,128)S(1)}, ...), branch_computations={%region_0.0_spmd, %region_1.0_spmd, %region_2.5_spmd} | conditional | flops 393282 | bytes 26740038 | solution.py:421
  45.9 2.6 %collect.7 = f32[3,8,8,512]{3,2,1,0:T(8,128)} custom-call(s32[24,8,128]{2,1,0:T(8,128)S(1)} %get-tuple-element.606.refs_0_, f32[2,3,256,128]{3,2,1,0:T(8,128)S(1)} %get-tuple-element.607.refs_1_, f32[2,3,256,128]{3,2,1,0:T(8,128)S(1)} %get-tuple-element.608.refs_2_, f32[3,128,128]{2,1,0:T(8,128)S(1)} %get-tuple-element.610.refs_4_.refs_3_, ...), custom_call_target="tpu_custom_call" | custom-call | flops 98304 | bytes 1179648 | tf_op jit(solution)/shard_map/cond/branch_0_fun/collect/pallas_call | solution.py:231
  48.5 2.8 %collect.6 = f32[4,8,8,512]{3,2,1,0:T(8,128)} custom-call(s32[24,8,128]{2,1,0:T(8,128)S(1)} %get-tuple-element.606.refs_0_, f32[2,3,256,128]{3,2,1,0:T(8,128)S(1)} %get-tuple-element.607.refs_1_, f32[2,3,256,128]{3,2,1,0:T(8,128)S(1)} %get-tuple-element.608.refs_2_, f32[256,128]{1,0:T(8,128)} %bitcast.2.refs_3_, ...), custom_call_target="tpu_custom_call" | custom-call | flops 98304 | bytes 1179648 | tf_op jit(solution)/shard_map/cond/branch_0_fun/collect/pallas_call | solution.py:231
  53.2 2.4 %collective-permute-start.23 = (f32[4,8,8,512]{3,2,1,0:T(8,128)}, f32[4,8,8,512]{3,2,1,0:T(8,128)S(1)}, u32[]{:S(2)}, u32[]{:S(2)}) collective-permute-start(f32[4,8,8,512]{3,2,1,0:T(8,128)} %get-tuple-element.689.refs_5_.refs_2_), channel_id=1, source_target_pairs={{0,1},{1,2},{2,3},{3,4},{4,5},{5,6},{6,7},{7,8},{8,9},{9,10},{10,1... | collective-permute-start | bytes 1572872 | tf_op jit(solution)/shard_map/ppermute | solution.py:35
  55.6 5.3 %collective-permute-start.22 = (f32[3,8,8,512]{3,2,1,0:T(8,128)}, f32[3,8,8,512]{3,2,1,0:T(8,128)S(1)}, u32[]{:S(2)}, u32[]{:S(2)}) collective-permute-start(f32[3,8,8,512]{3,2,1,0:T(8,128)} %get-tuple-element.688.refs_2_), channel_id=1, source_target_pairs={{1,0},{2,1},{3,2},{4,3},{5,4},{6,5},{7,6},{8,7},{9,8},{10,9},{11,1... | collective-permute-start | bytes 1179656 | tf_op jit(solution)/shard_map/ppermute | solution.py:35
  62.9 3.2 %collective-permute-done.23.refs_4_.refs_1_ = f32[4,8,8,512]{3,2,1,0:T(8,128)S(1)} collective-permute-done((f32[4,8,8,512]{3,2,1,0:T(8,128)}, f32[4,8,8,512]{3,2,1,0:T(8,128)S(1)}, u32[]{:S(2)}, u32[]{:S(2)}) %collective-permute-start.23) | collective-permute-done | bytes 524320 | tf_op jit(solution)/shard_map/ppermute | solution.py:35
  66.1 3.4 %advance.5.refs_2_ = f32[3,8,8,512]{3,2,1,0:T(8,128)S(1)} custom-call(s32[1]{0:T(128)} %bitcast.21.refs_0_, f32[4,8,8,512]{3,2,1,0:T(8,128)S(1)} %collective-permute-done.23.refs_4_.refs_1_, f32[4,8,8,512]{3,2,1,0:T(8,128)} %get-tuple-element.689.refs_5_.refs_2_, f32[4,8,8,512]{3,2,1,0:T(8,128)S(1)} %collective-permute-done.24.refs_6_.refs_3_, ...), custom_call_target="tpu_custom_call" | custom-call | flops 18874368 | bytes 1966080 | tf_op jit(solution)/shard_map/advance/pallas_call | solution.py:358
  69.4 2.6 %collective-permute-start.28 = (f32[3,8,8,512]{3,2,1,0:T(8,128)S(1)}, f32[3,8,8,512]{3,2,1,0:T(8,128)S(1)}, u32[]{:S(2)}, u32[]{:S(2)}) collective-permute-start(f32[3,8,8,512]{3,2,1,0:T(8,128)S(1)} %advance.5.refs_2_), channel_id=1, source_target_pairs={{1,0},{2,1},{3,2},{4,3},{5,4},{6,5},{7,6},{8,7},{9,8},{10,9},{11,1... | collective-permute-start | bytes 1179656 | tf_op jit(solution)/shard_map/ppermute | solution.py:35
  72.0 2.1 %collective-permute-start.27 = (f32[3,8,8,512]{3,2,1,0:T(8,128)S(1)}, f32[3,8,8,512]{3,2,1,0:T(8,128)S(1)}, u32[]{:S(2)}, u32[]{:S(2)}) collective-permute-start(f32[3,8,8,512]{3,2,1,0:T(8,128)S(1)} %advance.5.refs_2_), channel_id=1, source_target_pairs={{0,1},{1,2},{2,3},{3,4},{4,5},{5,6},{6,7},{7,8},{8,9},{9,10},{10,1... | collective-permute-start | bytes 1179656 | tf_op jit(solution)/shard_map/ppermute | solution.py:35
  74.2 3.3 %advance.4.refs_2_ = f32[3,8,8,512]{3,2,1,0:T(8,128)S(1)} custom-call(s32[1]{0:T(128)} %bitcast.21.refs_0_, f32[3,8,8,512]{3,2,1,0:T(8,128)S(1)} %collective-permute-done.21.refs_1_, f32[3,8,8,512]{3,2,1,0:T(8,128)} %get-tuple-element.688.refs_2_, f32[3,8,8,512]{3,2,1,0:T(8,128)S(1)} %collective-permute-done.22.refs_3_, ...), custom_call_target="tpu_custom_call" | custom-call | flops 18874368 | bytes 1966080 | tf_op jit(solution)/shard_map/advance/pallas_call | solution.py:358
  77.5 5.8 %collective-permute-start.26 = (f32[3,8,8,512]{3,2,1,0:T(8,128)S(1)}, f32[3,8,8,512]{3,2,1,0:T(8,128)S(1)}, u32[]{:S(2)}, u32[]{:S(2)}) collective-permute-start(f32[3,8,8,512]{3,2,1,0:T(8,128)S(1)} %advance.4.refs_2_), channel_id=1, source_target_pairs={{1,0},{2,1},{3,2},{4,3},{5,4},{6,5},{7,6},{8,7},{9,8},{10,9},{11,1... | collective-permute-start | bytes 1179656 | tf_op jit(solution)/shard_map/ppermute | solution.py:35
  85.2 4.1 %advance.6.refs_7_ = f32[2,3,256,128]{3,2,1,0:T(8,128)} custom-call(s32[1]{0:T(128)} %bitcast.21.refs_0_, f32[3,8,8,512]{3,2,1,0:T(8,128)S(1)} %collective-permute-done.27.refs_1_, f32[3,8,8,512]{3,2,1,0:T(8,128)S(1)} %advance.5.refs_2_, f32[3,8,8,512]{3,2,1,0:T(8,128)S(1)} %collective-permute-done.28.refs_3_, ...), custom_call_target="tpu_custom_call" | custom-call | flops 18874368 | bytes 1966080 | tf_op jit(solution)/shard_map/advance/pallas_call | solution.py:358
  89.4 5.1 %collective-permute-done.25.refs_1_ = f32[3,8,8,512]{3,2,1,0:T(8,128)S(1)} collective-permute-done((f32[3,8,8,512]{3,2,1,0:T(8,128)S(1)}, f32[3,8,8,512]{3,2,1,0:T(8,128)S(1)}, u32[]{:S(2)}, u32[]{:S(2)}) %collective-permute-start.25) | collective-permute-done | bytes 393248 | tf_op jit(solution)/shard_map/ppermute | solution.py:35
  94.5 4.1 %advance.7 = f32[2,3,256,128]{3,2,1,0:T(8,128)} custom-call(s32[1]{0:T(128)} %bitcast.21.refs_0_, f32[3,8,8,512]{3,2,1,0:T(8,128)S(1)} %collective-permute-done.25.refs_1_, f32[3,8,8,512]{3,2,1,0:T(8,128)S(1)} %advance.4.refs_2_, f32[3,8,8,512]{3,2,1,0:T(8,128)S(1)} %collective-permute-done.26.refs_3_, ...), custom_call_target="tpu_custom_call", output_to_operand_aliasing={{}: (7, {})} | custom-call | flops 18874368 | bytes 1966080 | tf_op jit(solution)/shard_map/advance/pallas_call | solution.py:358
  (55 shorter events, 21.2 us)
Async XLA Ops:
  3.6 7.8 %collective-permute-start.5 = (f32[3,128,128]{2,1,0:T(8,128)S(1)}, f32[3,128,128]{2,1,0:T(8,128)S(1)}, u32[]{:S(2)}, u32[]{:S(2)}) collective-permute-start(f32[3,128,128]{2,1,0:T(8,128)S(1)} %select.74), channel_id=1, source_target_pairs={{0,32},{32,64},{64,96},{96,128},{128,160},{160,192},{192,224},{224... | collective-permute-start | bytes 589832 | tf_op jit(solution)/shard_map/ppermute | solution.py:35
  5.6 9.0 %collective-permute-start.9 = (f32[3,128,128]{2,1,0:T(8,128)S(1)}, f32[3,128,128]{2,1,0:T(8,128)S(1)}, u32[]{:S(2)}, u32[]{:S(2)}) collective-permute-start(f32[3,128,128]{2,1,0:T(8,128)S(1)} %select.78), channel_id=1, source_target_pairs={{0,224},{32,0},{64,32},{96,64},{128,96},{160,128},{192,160},{224,1... | collective-permute-start | bytes 589832 | tf_op jit(solution)/shard_map/ppermute | solution.py:35
  5.8 9.8 %collective-permute-start.13 = (f32[3,128,128]{2,1,0:T(8,128)S(1)}, f32[3,128,128]{2,1,0:T(8,128)S(1)}, u32[]{:S(2)}, u32[]{:S(2)}) collective-permute-start(f32[3,128,128]{2,1,0:T(8,128)S(1)} %select.82), channel_id=1, source_target_pairs={{0,32},{32,64},{64,96},{96,128},{128,160},{160,192},{192,224},{224... | collective-permute-start | bytes 589832 | tf_op jit(solution)/shard_map/ppermute | solution.py:35
  8.9 9.8 %collective-permute-start.17 = (f32[3,128,128]{2,1,0:T(8,128)S(1)}, f32[3,128,128]{2,1,0:T(8,128)S(1)}, u32[]{:S(2)}, u32[]{:S(2)}) collective-permute-start(f32[3,128,128]{2,1,0:T(8,128)S(1)} %select.86), channel_id=1, source_target_pairs={{0,224},{32,0},{64,32},{96,64},{128,96},{160,128},{192,160},{224,1... | collective-permute-start | bytes 589832 | tf_op jit(solution)/shard_map/ppermute | solution.py:35
  11.4 8.4 %collective-permute-start.6 = (f32[3,128,128]{2,1,0:T(8,128)S(1)}, f32[3,128,128]{2,1,0:T(8,128)S(1)}, u32[]{:S(2)}, u32[]{:S(2)}) collective-permute-start(f32[3,128,128]{2,1,0:T(8,128)S(1)} %select.75), channel_id=1, source_target_pairs={{0,32},{32,64},{64,96},{96,128},{128,160},{160,192},{192,224},{224... | collective-permute-start | bytes 589832 | tf_op jit(solution)/shard_map/ppermute | solution.py:35
  14.6 8.6 %collective-permute-start.10 = (f32[3,128,128]{2,1,0:T(8,128)S(1)}, f32[3,128,128]{2,1,0:T(8,128)S(1)}, u32[]{:S(2)}, u32[]{:S(2)}) collective-permute-start(f32[3,128,128]{2,1,0:T(8,128)S(1)} %select.79), channel_id=1, source_target_pairs={{0,224},{32,0},{64,32},{96,64},{128,96},{160,128},{192,160},{224,1... | collective-permute-start | bytes 589832 | tf_op jit(solution)/shard_map/ppermute | solution.py:35
  15.7 8.4 %collective-permute-start.14 = (f32[3,128,128]{2,1,0:T(8,128)S(1)}, f32[3,128,128]{2,1,0:T(8,128)S(1)}, u32[]{:S(2)}, u32[]{:S(2)}) collective-permute-start(f32[3,128,128]{2,1,0:T(8,128)S(1)} %select.83), channel_id=1, source_target_pairs={{0,32},{32,64},{64,96},{96,128},{128,160},{160,192},{192,224},{224... | collective-permute-start | bytes 589832 | tf_op jit(solution)/shard_map/ppermute | solution.py:35
  18.8 9.1 %collective-permute-start.18 = (f32[3,128,128]{2,1,0:T(8,128)S(1)}, f32[3,128,128]{2,1,0:T(8,128)S(1)}, u32[]{:S(2)}, u32[]{:S(2)}) collective-permute-start(f32[3,128,128]{2,1,0:T(8,128)S(1)} %select.87), channel_id=1, source_target_pairs={{0,224},{32,0},{64,32},{96,64},{128,96},{160,128},{192,160},{224,1... | collective-permute-start | bytes 589832 | tf_op jit(solution)/shard_map/ppermute | solution.py:35
  19.9 8.4 %collective-permute-start.7 = (f32[3,128,128]{2,1,0:T(8,128)S(1)}, f32[3,128,128]{2,1,0:T(8,128)S(1)}, u32[]{:S(2)}, u32[]{:S(2)}) collective-permute-start(f32[3,128,128]{2,1,0:T(8,128)S(1)} %select.76), channel_id=1, source_target_pairs={{0,32},{32,64},{64,96},{96,128},{128,160},{160,192},{192,224},{224... | collective-permute-start | bytes 589832 | tf_op jit(solution)/shard_map/ppermute | solution.py:35
  23.2 9.1 %collective-permute-start.11 = (f32[3,128,128]{2,1,0:T(8,128)S(1)}, f32[3,128,128]{2,1,0:T(8,128)}, u32[]{:S(2)}, u32[]{:S(2)}) collective-permute-start(f32[3,128,128]{2,1,0:T(8,128)S(1)} %select.80), channel_id=1, source_target_pairs={{0,224},{32,0},{64,32},{96,64},{128,96},{160,128},{192,160},{224,1... | collective-permute-start | bytes 589832 | tf_op jit(solution)/shard_map/ppermute | solution.py:35
  24.1 9.3 %collective-permute-start.15 = (f32[3,128,128]{2,1,0:T(8,128)S(1)}, f32[3,128,128]{2,1,0:T(8,128)}, u32[]{:S(2)}, u32[]{:S(2)}) collective-permute-start(f32[3,128,128]{2,1,0:T(8,128)S(1)} %select.84), channel_id=1, source_target_pairs={{0,32},{32,64},{64,96},{96,128},{128,160},{160,192},{192,224},{224... | collective-permute-start | bytes 589832 | tf_op jit(solution)/shard_map/ppermute | solution.py:35
  27.9 10.0 %collective-permute-start.19 = (f32[3,128,128]{2,1,0:T(8,128)S(1)}, f32[3,128,128]{2,1,0:T(8,128)}, u32[]{:S(2)}, u32[]{:S(2)}) collective-permute-start(f32[3,128,128]{2,1,0:T(8,128)S(1)} %select.88), channel_id=1, source_target_pairs={{0,224},{32,0},{64,32},{96,64},{128,96},{160,128},{192,160},{224,1... | collective-permute-start | bytes 589832 | tf_op jit(solution)/shard_map/ppermute | solution.py:35
  28.3 11.8 %collective-permute-start.8 = (f32[3,128,128]{2,1,0:T(8,128)S(1)}, f32[3,128,128]{2,1,0:T(8,128)}, u32[]{:S(2)}, u32[]{:S(2)}) collective-permute-start(f32[3,128,128]{2,1,0:T(8,128)S(1)} %select.77), channel_id=1, source_target_pairs={{0,32},{32,64},{64,96},{96,128},{128,160},{160,192},{192,224},{224... | collective-permute-start | bytes 589832 | tf_op jit(solution)/shard_map/ppermute | solution.py:35
  33.3 9.0 %collective-permute-start.12 = (f32[3,128,128]{2,1,0:T(8,128)S(1)}, f32[3,128,128]{2,1,0:T(8,128)}, u32[]{:S(2)}, u32[]{:S(2)}) collective-permute-start(f32[3,128,128]{2,1,0:T(8,128)S(1)} %select.81), channel_id=1, source_target_pairs={{0,224},{32,0},{64,32},{96,64},{128,96},{160,128},{192,160},{224,1... | collective-permute-start | bytes 589832 | tf_op jit(solution)/shard_map/ppermute | solution.py:35
  34.4 7.9 %collective-permute-start.16 = (f32[3,128,128]{2,1,0:T(8,128)S(1)}, f32[3,128,128]{2,1,0:T(8,128)}, u32[]{:S(2)}, u32[]{:S(2)}) collective-permute-start(f32[3,128,128]{2,1,0:T(8,128)S(1)} %select.85), channel_id=1, source_target_pairs={{0,32},{32,64},{64,96},{96,128},{128,160},{160,192},{192,224},{224... | collective-permute-start | bytes 589832 | tf_op jit(solution)/shard_map/ppermute | solution.py:35
  38.9 7.0 %collective-permute-start.20 = (f32[3,128,128]{2,1,0:T(8,128)S(1)}, f32[3,128,128]{2,1,0:T(8,128)}, u32[]{:S(2)}, u32[]{:S(2)}) collective-permute-start(f32[3,128,128]{2,1,0:T(8,128)S(1)} %select.89), channel_id=1, source_target_pairs={{0,224},{32,0},{64,32},{96,64},{128,96},{160,128},{192,160},{224,1... | collective-permute-start | bytes 589832 | tf_op jit(solution)/shard_map/ppermute | solution.py:35
  51.3 11.5 %collective-permute-start.24 = (f32[4,8,8,512]{3,2,1,0:T(8,128)}, f32[4,8,8,512]{3,2,1,0:T(8,128)S(1)}, u32[]{:S(2)}, u32[]{:S(2)}) collective-permute-start(f32[4,8,8,512]{3,2,1,0:T(8,128)} %get-tuple-element.689.refs_5_.refs_2_), channel_id=1, source_target_pairs={{1,0},{2,1},{3,2},{4,3},{5,4},{6,5},{7,6},{8,7},{9,8},{10,9},{11,1... | collective-permute-start | bytes 1572872 | tf_op jit(solution)/shard_map/ppermute | solution.py:35
  53.2 12.8 %collective-permute-start.23 = (f32[4,8,8,512]{3,2,1,0:T(8,128)}, f32[4,8,8,512]{3,2,1,0:T(8,128)S(1)}, u32[]{:S(2)}, u32[]{:S(2)}) collective-permute-start(f32[4,8,8,512]{3,2,1,0:T(8,128)} %get-tuple-element.689.refs_5_.refs_2_), channel_id=1, source_target_pairs={{0,1},{1,2},{2,3},{3,4},{4,5},{5,6},{6,7},{7,8},{8,9},{9,10},{10,1... | collective-permute-start | bytes 1572872 | tf_op jit(solution)/shard_map/ppermute | solution.py:35
  55.6 18.5 %collective-permute-start.22 = (f32[3,8,8,512]{3,2,1,0:T(8,128)}, f32[3,8,8,512]{3,2,1,0:T(8,128)S(1)}, u32[]{:S(2)}, u32[]{:S(2)}) collective-permute-start(f32[3,8,8,512]{3,2,1,0:T(8,128)} %get-tuple-element.688.refs_2_), channel_id=1, source_target_pairs={{1,0},{2,1},{3,2},{4,3},{5,4},{6,5},{7,6},{8,7},{9,8},{10,9},{11,1... | collective-permute-start | bytes 1179656 | tf_op jit(solution)/shard_map/ppermute | solution.py:35
  60.9 13.3 %collective-permute-start.21 = (f32[3,8,8,512]{3,2,1,0:T(8,128)}, f32[3,8,8,512]{3,2,1,0:T(8,128)S(1)}, u32[]{:S(2)}, u32[]{:S(2)}) collective-permute-start(f32[3,8,8,512]{3,2,1,0:T(8,128)} %get-tuple-element.688.refs_2_), channel_id=1, source_target_pairs={{0,1},{1,2},{2,3},{3,4},{4,5},{5,6},{6,7},{7,8},{8,9},{9,10},{10,1... | collective-permute-start | bytes 1179656 | tf_op jit(solution)/shard_map/ppermute | solution.py:35
  69.4 15.8 %collective-permute-start.28 = (f32[3,8,8,512]{3,2,1,0:T(8,128)S(1)}, f32[3,8,8,512]{3,2,1,0:T(8,128)S(1)}, u32[]{:S(2)}, u32[]{:S(2)}) collective-permute-start(f32[3,8,8,512]{3,2,1,0:T(8,128)S(1)} %advance.5.refs_2_), channel_id=1, source_target_pairs={{1,0},{2,1},{3,2},{4,3},{5,4},{6,5},{7,6},{8,7},{9,8},{10,9},{11,1... | collective-permute-start | bytes 1179656 | tf_op jit(solution)/shard_map/ppermute | solution.py:35
  72.0 13.2 %collective-permute-start.27 = (f32[3,8,8,512]{3,2,1,0:T(8,128)S(1)}, f32[3,8,8,512]{3,2,1,0:T(8,128)S(1)}, u32[]{:S(2)}, u32[]{:S(2)}) collective-permute-start(f32[3,8,8,512]{3,2,1,0:T(8,128)S(1)} %advance.5.refs_2_), channel_id=1, source_target_pairs={{0,1},{1,2},{2,3},{3,4},{4,5},{5,6},{6,7},{7,8},{8,9},{9,10},{10,1... | collective-permute-start | bytes 1179656 | tf_op jit(solution)/shard_map/ppermute | solution.py:35
  77.5 11.8 %collective-permute-start.26 = (f32[3,8,8,512]{3,2,1,0:T(8,128)S(1)}, f32[3,8,8,512]{3,2,1,0:T(8,128)S(1)}, u32[]{:S(2)}, u32[]{:S(2)}) collective-permute-start(f32[3,8,8,512]{3,2,1,0:T(8,128)S(1)} %advance.4.refs_2_), channel_id=1, source_target_pairs={{1,0},{2,1},{3,2},{4,3},{5,4},{6,5},{7,6},{8,7},{9,8},{10,9},{11,1... | collective-permute-start | bytes 1179656 | tf_op jit(solution)/shard_map/ppermute | solution.py:35
  83.3 11.2 %collective-permute-start.25 = (f32[3,8,8,512]{3,2,1,0:T(8,128)S(1)}, f32[3,8,8,512]{3,2,1,0:T(8,128)S(1)}, u32[]{:S(2)}, u32[]{:S(2)}) collective-permute-start(f32[3,8,8,512]{3,2,1,0:T(8,128)S(1)} %advance.4.refs_2_), channel_id=1, source_target_pairs={{0,1},{1,2},{2,3},{3,4},{4,5},{5,6},{6,7},{7,8},{8,9},{9,10},{10,1... | collective-permute-start | bytes 1179656 | tf_op jit(solution)/shard_map/ppermute | solution.py:35
  (3 other events, 13.3 us)
